TPU v7x, 256 devices: a whole 4x4x8 slice. The times are simulated.
256 devices in a mesh: frame: 64 (over y, x_lo, z), head: 4 (over x_hi, core).
Axes of the slice: x: 4 (x_hi: 2, x_lo: 2; x = x_hi * 2 + x_lo), y: 4, z: 8, core: 2. Of those that a mesh axis runs over, the one named last changes fastest.
Arguments:
- latents: bfloat16 [32768, 5120], P('frame', 'head'), may hold values from -6 to 6
- queries: bfloat16 [32768, 2560], P('frame', 'head'), may hold values from -22 to 22
- keys: bfloat16 [32768, 2560], P('frame', 'head'), may hold values from -6 to 6
- values: bfloat16 [32768, 2560], P('frame', 'head'), may hold values from -6 to 6
- out_weight: bfloat16 [2560, 5120], P('head'), may hold values from -0.5 to 0.5
- gate_table: float32 [4, 5120], P(None, 'head'), may hold values from 0.5 to 2
- levels: int32 [64], P('frame'), may hold values from 0 to 3
- block_mask: int32 [64, 4], P('frame'), may hold values from 0 to 1, as said below
- fresh: bfloat16 [512, 5120], P(None, 'head'), may hold values from -6 to 6
Outputs:
- velocity: bfloat16 [32768, 5120], P('frame', 'head')
- next_latents: bfloat16 [32768, 5120], P('frame', 'head')
Inputs may be any that keep to these rules, and one draw needn't show every extreme that they name: block_mask[c, 0] is 1 for every span c.
All inputs are finite; a program needn't handle non-finite values.
Results may differ from a plain program's by a relative error of at most 0.012.
Values may be sent and summed in bfloat16 or wider, within the bound.
No kernel may reach another device: no remote copies, remote signals or barrier semaphores. Data moves between devices by JAX's collectives and lax.ppermute only.
A program may use at most 128 MiB of HBM per device.

v0:
```python
import math

import jax
import jax.numpy as jnp
from jax import lax
from jax.sharding import PartitionSpec as P

HD = 128
LEVELS = 4


flow_shift = 5.0


def shifted(value, axis, by):
    devices = lax.axis_size(axis)
    pairs = [(i, i + by) for i in range(devices) if 0 <= i + by < devices]
    return lax.ppermute(value, axis, pairs)


def split_up(value, dim, devices):
    before, after = (value.shape[:dim], value.shape[dim + 1 :])
    return jnp.moveaxis(value.reshape(*before, devices, -1, *after), dim, 0)


def sent_and_summed(value, axis, dim):
    tiles = split_up(value, dim, lax.axis_size(axis))
    arrived = lax.all_to_all(tiles, axis, split_axis=0, concat_axis=0, tiled=True)
    return arrived.astype(jnp.float32).sum(axis=0)


def noise_level(point):
    return flow_shift * point / (1.0 + (flow_shift - 1.0) * point)


def shards(latents, queries, keys, values, out_weight, gate_table, levels, block_mask, fresh):
    rows_here = queries.shape[0]
    width_here = queries.shape[1]
    heads_here = width_here // HD
    window = block_mask.shape[1]
    key_list = [keys]
    value_list = [values]
    carried = (keys, values)
    for distance in range(1, window):
        carried = shifted((carried[0], carried[1]), "frame", 1)
        key_list.append(carried[0])
        value_list.append(carried[1])
    key_stack = jnp.stack(key_list, 0)
    value_stack = jnp.stack(value_list, 0)
    position = lax.axis_index("frame")
    distances = jnp.arange(window, dtype=jnp.int32)
    allowed = (block_mask[0] == 1) & (position - distances >= 0)
    scale = 1.0 / math.sqrt(HD)
    query_heads = queries.reshape(rows_here, heads_here, HD)
    key_heads = key_stack.reshape(window, rows_here, heads_here, HD)
    value_heads = value_stack.reshape(window, rows_here, heads_here, HD)
    scores = (
        jnp.einsum("qhd,bkhd->hqbk", query_heads, key_heads, preferred_element_type=jnp.float32)
        * scale
    )
    scores = jnp.where(allowed[None, None, :, None], scores, -jnp.inf)
    top = jnp.max(scores, axis=(2, 3), keepdims=True)
    expd = jnp.exp(scores - top)
    weights = (expd / jnp.sum(expd, axis=(2, 3), keepdims=True)).astype(jnp.bfloat16)
    attended = jnp.einsum(
        "hqbk,bkhd->qhd", weights, value_heads, preferred_element_type=jnp.float32
    )
    attended = attended.reshape(rows_here, width_here).astype(jnp.bfloat16)
    partial_value = jnp.dot(attended, out_weight, preferred_element_type=jnp.float32)
    projected = sent_and_summed(partial_value.astype(jnp.bfloat16), "head", 1)
    level_value = levels[0]
    picker = (jnp.arange(LEVELS, dtype=jnp.int32) == level_value).astype(jnp.float32)
    gate = jnp.dot(picker, gate_table, precision=lax.Precision.HIGHEST)
    level_float = level_value.astype(jnp.float32)
    delta = noise_level(level_float / LEVELS) - noise_level((level_float + 1.0) / LEVELS)
    gated = gate[None, :] * projected
    velocity = gated.astype(jnp.bfloat16)
    update = delta * gated
    updated = (latents.astype(jnp.float32) + update).astype(jnp.bfloat16)
    moved = shifted(updated, "frame", -1)
    is_last = position == lax.axis_size("frame") - 1
    next_latents = jnp.where(is_last, fresh, moved)
    return (velocity, next_latents)


def solution(mesh):
    in_specs = (
        P("frame", "head"),
        P("frame", "head"),
        P("frame", "head"),
        P("frame", "head"),
        P("head", None),
        P(None, "head"),
        P("frame"),
        P("frame", None),
        P(None, "head"),
    )
    out_specs = (P("frame", "head"), P("frame", "head"))
    return jax.shard_map(shards, mesh=mesh, in_specs=in_specs, out_specs=out_specs, check_vma=False)
```

profile of v0, /device:TPU:9, one launch (start us, length us, event | category | flops | bytes accessed | tf_op | source)
XLA Modules:
  0.0 221.9 jit_solution(15103510897952254881)
XLA Ops:
  2.0 3.5 %collective-permute-start.3 = (bf16[512,640]{0,1:T(8,128)(2,1)S(1)}, bf16[512,640]{0,1:T(8,128)(2,1)S(1)}, u32[]{:S(2)}, u32[]{:S(2)}) collective-permute-start(bf16[512,640]{0,1:T(8,128)(2,1)S(1)} %copy.34), channel_id=1, source_target_pairs={{0,4},{4,8},{8,12},{12,16},{16,20},{20,24},{24,28},{28,32},{32,36}... | collective-permute-start | bytes 1966088 | tf_op jit(solution)/shard_map/ppermute | solution.py:18
  5.6 3.5 %collective-permute-start = (bf16[512,640]{1,0:T(8,128)(2,1)}, bf16[512,640]{1,0:T(8,128)(2,1)}, u32[]{:S(2)}, u32[]{:S(2)}) collective-permute-start(bf16[512,640]{1,0:T(8,128)(2,1)} %param.12), channel_id=1, source_target_pairs={{0,4},{4,8},{8,12},{12,16},{16,20},{20,24},{24,28},{28,32},{32,36}... | collective-permute-start | bytes 1966088 | tf_op jit(solution)/shard_map/ppermute | solution.py:18
  9.1 15.6 %collective-permute-done.3 = bf16[512,640]{0,1:T(8,128)(2,1)S(1)} collective-permute-done((bf16[512,640]{0,1:T(8,128)(2,1)S(1)}, bf16[512,640]{0,1:T(8,128)(2,1)S(1)}, u32[]{:S(2)}, u32[]{:S(2)}) %collective-permute-start.3) | collective-permute-done | bytes 655392 | tf_op jit(solution)/shard_map/ppermute | solution.py:18
  24.8 1.9 collective-permute-start.4
  26.7 12.2 %collective-permute-done = bf16[512,640]{1,0:T(8,128)(2,1)} collective-permute-done((bf16[512,640]{1,0:T(8,128)(2,1)}, bf16[512,640]{1,0:T(8,128)(2,1)}, u32[]{:S(2)}, u32[]{:S(2)}) %collective-permute-start) | collective-permute-done | bytes 655392 | tf_op jit(solution)/shard_map/ppermute | solution.py:18
  38.9 1.9 collective-permute-start.1
  40.8 12.0 %collective-permute-done.4 = bf16[512,640]{0,1:T(8,128)(2,1)S(1)} collective-permute-done((bf16[512,640]{0,1:T(8,128)(2,1)S(1)}, bf16[512,640]{0,1:T(8,128)(2,1)S(1)}, u32[]{:S(2)}, u32[]{:S(2)}) %collective-permute-start.4) | collective-permute-done | bytes 655392 | tf_op jit(solution)/shard_map/ppermute | solution.py:18
  52.8 1.9 collective-permute-start.5
  57.2 2.2 copy.40
  62.9 4.0 %collective-permute-done.1 = bf16[512,640]{1,0:T(8,128)(2,1)S(1)} collective-permute-done((bf16[512,640]{1,0:T(8,128)(2,1)}, bf16[512,640]{1,0:T(8,128)(2,1)S(1)}, u32[]{:S(2)}, u32[]{:S(2)}) %collective-permute-start.1) | collective-permute-done | bytes 655392 | tf_op jit(solution)/shard_map/ppermute | solution.py:18
  66.9 1.9 collective-permute-start.2
  69.1 12.0 %collective-permute-done.5 = bf16[512,640]{0,1:T(8,128)(2,1)} collective-permute-done((bf16[512,640]{0,1:T(8,128)(2,1)S(1)}, bf16[512,640]{0,1:T(8,128)(2,1)}, u32[]{:S(2)}, u32[]{:S(2)}) %collective-permute-start.5) | collective-permute-done | bytes 655392 | tf_op jit(solution)/shard_map/ppermute | solution.py:18
  82.4 4.5 %bitcast_reduce_fusion = (f32[5,512]{1,0:T(8,128)S(1)}, f32[5,4,512,512]{3,2,1,0:T(8,128)S(1)}) fusion(pred[4]{0:T(512)(128)(4,1)S(1)} %bitcast_and_fusion, bf16[512,5,128,1]{0,2,3,1:T(8,128)(2,1)} %bitcast.62, bf16[1,512,5,128]{3,1,0,2:T(8,128)(2,1)S(1)} %copy.39, bf16[1,512,5,128]{3,1,0,2:T(8,128)(2,1)} %copy.38, bf16[1,512,5,128]{3,1,0,2:T(8,128)(2,1)} %copy.37, ...), kind=kOutput, calls=%fused_computation.1 | convolution fusion | flops 1361835520 | bytes 24258564 | tf_op jit(solution)/shard_map/qhd,bkhd->hqbk/dot_general | solution.py:58
  87.0 4.7 %fusion.1 = f32[5,512]{1,0:T(8,128)S(1)} fusion(f32[5,4,512,512]{3,2,1,0:T(8,128)S(1)} %get-tuple-element.5, f32[5,512]{1,0:T(8,128)S(1)} %get-tuple-element.4, pred[4]{0:T(512)(128)(4,1)S(1)} %bitcast_and_fusion), kind=kLoop, calls=%fused_computation.5 | loop fusion | flops 20968960 | bytes 20992004 | tf_op jit(solution)/shard_map/reduce_sum | solution.py:64
  91.6 2.3 %copy-done.1 = f32[5,4,512,512]{3,2,1,0:T(8,128)} copy-done((f32[5,4,512,512]{3,2,1,0:T(8,128)}, f32[5,4,512,512]{3,2,1,0:T(8,128)S(1)}, u32[]{:S(2)}) %copy-start.1) | copy-done | bytes 20971544
  96.4 10.7 %fusion.21 = bf16[5,128,512]{2,1,0:T(8,128)(2,1)S(1)} fusion(f32[5,4,512,512]{3,2,1,0:T(8,128)} %copy-done.1, f32[5,512]{1,0:T(8,128)S(1)} %fusion.1, f32[5,512]{1,0:T(8,128)S(1)} %get-tuple-element.4, pred[4]{0:T(512)(128)(4,1)S(1)} %bitcast_and_fusion, bf16[1,512,5,128]{1,3,0,2:T(8,128)(2,1)S(1)} %bitcast.63, bf16[1,512,5,128]{1,3,0,2:T(8,128)(2,1)S(1)} %bitcast.61, ...), kind=kOutput, calls=%fused_computation.28 | convolution fusion | flops 1372651520 | bytes 24268804 | tf_op jit(solution)/shard_map/hqbk,bkhd->qhd/dot_general | solution.py:65
  107.1 7.4 %convolution_convert_fusion = bf16[512,5120]{1,0:T(8,128)(2,1)S(1)} fusion(bf16[512,640]{0,1:T(8,128)(2,1)S(1)} %bitcast.64, bf16[640,5120]{1,0:T(8,128)(2,1)} %param.13), kind=kOutput, calls=%fused_computation.8 | convolution fusion | flops 3358064640 | bytes 12451840 | tf_op jit(solution)/shard_map/dot_general | solution.py:69
  114.5 2.7 %copy.51 = bf16[64,4,8,1280]{3,2,0,1:T(8,128)(2,1)} copy(bf16[64,4,8,1280]{3,2,1,0:T(8,128)(2,1)S(1)} %bitcast.55) | data formatting | bytes 10485760 | tf_op jit(solution)/shard_map/reshape | solution.py:23
  117.2 6.2 %all-to-all-start = ((bf16[4,512,1280]{2,1,0:T(8,128)(2,1)}), bf16[4,512,1280]{2,1,0:T(8,128)(2,1)}, u32[]{:S(2)}, u32[]{:S(2)}) async-start(bf16[4,512,1280]{2,1,0:T(8,128)(2,1)} %bitcast.54), calls=%async_computation | async-start | bytes 10485760 | tf_op jit(solution)/shard_map/all_to_all | solution.py:28
  124.4 59.1 %all-to-all-done = bf16[4,512,1280]{2,1,0:T(8,128)(2,1)} async-done(((bf16[4,512,1280]{2,1,0:T(8,128)(2,1)}), bf16[4,512,1280]{2,1,0:T(8,128)(2,1)}, u32[]{:S(2)}, u32[]{:S(2)}) %all-to-all-start) | async-done | bytes 5242912 | tf_op jit(solution)/shard_map/all_to_all | solution.py:28
  183.6 3.6 %convert_reduce_fusion = f32[512,1280]{1,0:T(8,128)S(1)} fusion(bf16[4,512,1280]{2,1,0:T(8,128)(2,1)} %all-to-all-done), kind=kLoop, calls=%fused_computation.6 | loop fusion | flops 4587520 | bytes 7864320 | tf_op jit(solution)/shard_map/reduce_sum | solution.py:29
  187.2 2.0 add_convert_fusion
  189.2 3.3 %collective-permute-start.6 = (bf16[512,1280]{1,0:T(8,128)(2,1)}, bf16[512,1280]{1,0:T(8,128)(2,1)S(1)}, u32[]{:S(2)}, u32[]{:S(2)}) collective-permute-start(bf16[512,1280]{1,0:T(8,128)(2,1)} %get-tuple-element.2), channel_id=1, source_target_pairs={{4,0},{8,4},{12,8},{16,12},{20,16},{24,20},{28,24},{32,28},{36,32}... | collective-permute-start | bytes 3932168 | tf_op jit(solution)/shard_map/ppermute | solution.py:18
  192.6 28.1 %collective-permute-done.6 = bf16[512,1280]{1,0:T(8,128)(2,1)S(1)} collective-permute-done((bf16[512,1280]{1,0:T(8,128)(2,1)}, bf16[512,1280]{1,0:T(8,128)(2,1)S(1)}, u32[]{:S(2)}, u32[]{:S(2)}) %collective-permute-start.6) | collective-permute-done | bytes 1310752 | tf_op jit(solution)/shard_map/ppermute | solution.py:18
  (22 shorter events, 12.8 us)
Async XLA Ops:
  0.6 123.6 %copy-start = (f32[4,1280]{1,0:T(4,128)S(1)}, f32[4,1280]{1,0:T(4,128)}, u32[]{:S(2)}) copy-start(f32[4,1280]{1,0:T(4,128)} %param.14) | copy-start | bytes 61444
  0.6 58.7 %copy-start.4 = (s32[1,4]{1,0:T(1,128)S(1)}, s32[1,4]{1,0:T(1,128)}, u32[]{:S(2)}) copy-start(s32[1,4]{1,0:T(1,128)} %param.16) | copy-start | bytes 52
  2.0 22.7 %collective-permute-start.3 = (bf16[512,640]{0,1:T(8,128)(2,1)S(1)}, bf16[512,640]{0,1:T(8,128)(2,1)S(1)}, u32[]{:S(2)}, u32[]{:S(2)}) collective-permute-start(bf16[512,640]{0,1:T(8,128)(2,1)S(1)} %copy.34), channel_id=1, source_target_pairs={{0,4},{4,8},{8,12},{12,16},{16,20},{20,24},{24,28},{28,32},{32,36}... | collective-permute-start | bytes 1966088 | tf_op jit(solution)/shard_map/ppermute | solution.py:18
  5.6 33.3 %collective-permute-start = (bf16[512,640]{1,0:T(8,128)(2,1)}, bf16[512,640]{1,0:T(8,128)(2,1)}, u32[]{:S(2)}, u32[]{:S(2)}) collective-permute-start(bf16[512,640]{1,0:T(8,128)(2,1)} %param.12), channel_id=1, source_target_pairs={{0,4},{4,8},{8,12},{12,16},{16,20},{20,24},{24,28},{28,32},{32,36}... | collective-permute-start | bytes 1966088 | tf_op jit(solution)/shard_map/ppermute | solution.py:18
  24.8 28.1 %collective-permute-start.4 = (bf16[512,640]{0,1:T(8,128)(2,1)S(1)}, bf16[512,640]{0,1:T(8,128)(2,1)S(1)}, u32[]{:S(2)}, u32[]{:S(2)}) collective-permute-start(bf16[512,640]{0,1:T(8,128)(2,1)S(1)} %collective-permute-done.3), channel_id=1, source_target_pairs={{0,4},{4,8},{8,12},{12,16},{16,20},{20,24},{24,28},{28,32},{32,36}... | collective-permute-start | bytes 1966088 | tf_op jit(solution)/shard_map/ppermute | solution.py:18
  38.9 28.0 %collective-permute-start.1 = (bf16[512,640]{1,0:T(8,128)(2,1)}, bf16[512,640]{1,0:T(8,128)(2,1)S(1)}, u32[]{:S(2)}, u32[]{:S(2)}) collective-permute-start(bf16[512,640]{1,0:T(8,128)(2,1)} %collective-permute-done), channel_id=1, source_target_pairs={{0,4},{4,8},{8,12},{12,16},{16,20},{20,24},{24,28},{28,32},{32,36}... | collective-permute-start | bytes 1966088 | tf_op jit(solution)/shard_map/ppermute | solution.py:18
  52.8 28.2 %collective-permute-start.5 = (bf16[512,640]{0,1:T(8,128)(2,1)S(1)}, bf16[512,640]{0,1:T(8,128)(2,1)}, u32[]{:S(2)}, u32[]{:S(2)}) collective-permute-start(bf16[512,640]{0,1:T(8,128)(2,1)S(1)} %collective-permute-done.4), channel_id=1, source_target_pairs={{0,4},{4,8},{8,12},{12,16},{16,20},{20,24},{24,28},{28,32},{32,36}... | collective-permute-start | bytes 1966088 | tf_op jit(solution)/shard_map/ppermute | solution.py:18
  66.9 28.2 %collective-permute-start.2 = (bf16[512,640]{1,0:T(8,128)(2,1)S(1)}, bf16[512,640]{1,0:T(8,128)(2,1)}, u32[]{:S(2)}, u32[]{:S(2)}) collective-permute-start(bf16[512,640]{1,0:T(8,128)(2,1)S(1)} %collective-permute-done.1), channel_id=1, source_target_pairs={{0,4},{4,8},{8,12},{12,16},{16,20},{20,24},{24,28},{28,32},{32,36}... | collective-permute-start | bytes 1966088 | tf_op jit(solution)/shard_map/ppermute | solution.py:18
  87.0 7.0 %copy-start.1 = (f32[5,4,512,512]{3,2,1,0:T(8,128)}, f32[5,4,512,512]{3,2,1,0:T(8,128)S(1)}, u32[]{:S(2)}) copy-start(f32[5,4,512,512]{3,2,1,0:T(8,128)S(1)} %get-tuple-element.5) | copy-start | bytes 62914564
  117.2 66.4 %all-to-all-start = ((bf16[4,512,1280]{2,1,0:T(8,128)(2,1)}), bf16[4,512,1280]{2,1,0:T(8,128)(2,1)}, u32[]{:S(2)}, u32[]{:S(2)}) async-start(bf16[4,512,1280]{2,1,0:T(8,128)(2,1)} %bitcast.54), calls=%async_computation | async-start | bytes 10485760 | tf_op jit(solution)/shard_map/all_to_all | solution.py:28
  123.4 63.8 %copy-start.3 = (bf16[512,1280]{1,0:T(8,128)(2,1)S(1)}, bf16[512,1280]{1,0:T(8,128)(2,1)}, u32[]{:S(2)}) copy-start(bf16[512,1280]{1,0:T(8,128)(2,1)} %param.9) | copy-start | bytes 3932164
  187.2 33.5 %copy-start.2 = (bf16[512,1280]{1,0:T(8,128)(2,1)S(1)}, bf16[512,1280]{1,0:T(8,128)(2,1)}, u32[]{:S(2)}) copy-start(bf16[512,1280]{1,0:T(8,128)(2,1)} %param.17) | copy-start | bytes 3932164
  189.2 31.5 %collective-permute-start.6 = (bf16[512,1280]{1,0:T(8,128)(2,1)}, bf16[512,1280]{1,0:T(8,128)(2,1)S(1)}, u32[]{:S(2)}, u32[]{:S(2)}) collective-permute-start(bf16[512,1280]{1,0:T(8,128)(2,1)} %get-tuple-element.2), channel_id=1, source_target_pairs={{4,0},{8,4},{12,8},{16,12},{20,16},{24,20},{28,24},{32,28},{36,32}... | collective-permute-start | bytes 3932168 | tf_op jit(solution)/shard_map/ppermute | solution.py:18
where the time goes:
time: 224 us; the launch traced here: 222 us
  waiting for transfers between devices  144 us (64%)
  starting transfers between devices  24.3 us (11%)
  matrix products  22.8 us (10%)
  local copies, waits for them, and re-layouts  17.4 us (8%)
  other arithmetic  11.5 us (5%)
    ppermute x7, waiting for transfers between devices, shifted(): return lax.ppermute(value, axis, pairs)  85.2 us
    all_to_all x1, waiting for transfers between devices, sent_and_summed(): lax.all_to_all(tiles, axis, split_axis=0, concat_axis=0, tiled=True)  59.1 us
    ppermute x7, starting transfers between devices, shifted(): return lax.ppermute(value, axis, pairs)  18.1 us
    dot_general x1, matrix products, shards(): jnp.einsum('hqbk,bkhd->qhd', weights, value_heads, preferred_element_type...  10.7 us
    dot_general x1, matrix products, shards(): jnp.dot(attended, out_weight, preferred_element_type=jnp.float32)  7.4 us
    unnamed x13, local copies, waits for them, and re-layouts  7.16 us
    all_to_all x1, starting transfers between devices, sent_and_summed(): lax.all_to_all(tiles, axis, split_axis=0, concat_axis=0, tiled=True)  6.24 us
    reduce_sum x1, other arithmetic, shards(): jnp.sum(expd, axis=(2, 3), keepdims=True)  4.67 us
  transfers between devices with their start and end apart: 8, of which 8 were waited for; matrix products, arithmetic and copies ran while one was open for 9% of the time, Pallas kernels for 0%

commit v1 on v0

v1 whole, which is shorter than its diff:
```python
import math

import jax
import jax.numpy as jnp
import numpy as np
from jax import lax
from jax.experimental import pallas as pl
from jax.experimental.pallas import tpu as pltpu
from jax.sharding import PartitionSpec as P

HD = 128
LEVELS = 4
flow_shift = 5.0
C = math.log2(math.e) / math.sqrt(HD)
F32 = jnp.float32
BF16 = jnp.bfloat16
NY, NXL, NZ = 4, 2, 8
SIBLING = [(0, 1), (1, 0), (2, 3), (3, 2)]
PARTNER = [(0, 2), (2, 0), (1, 3), (3, 1)]


def noise_level(point):
    return flow_shift * point / (1.0 + (flow_shift - 1.0) * point)


def ring(value, by):
    n = lax.axis_size("frame")
    return lax.ppermute(value, "frame", [(i, (i + by) % n) for i in range(n)])


def swap(value, pairs):
    return lax.ppermute(value, "head", pairs)


NT = (((1,), (1,)), ((), ()))
ON_CHIP = pl.BlockSpec(memory_space=pltpu.VMEM)
SCALARS = pl.BlockSpec(memory_space=pltpu.SMEM)
CHUNK = 256


def attend_first(allow, q_ref, k0, v0, k1, v1, k2, v2, k3, acc_ref, p_ref):
    rows, width = q_ref.shape
    on = [jnp.where(allow[i] == 1, 1.0, 0.0) for i in range(4)]
    for h in range(width // HD):
        hs = pl.ds(h * HD, HD)
        for c in range(rows // CHUNK):
            cs = pl.ds(c * CHUNK, CHUNK)
            q = q_ref[cs, hs]
            s = [lax.dot_general(q, k[:, hs], NT, preferred_element_type=F32) for k in (k0, k1, k2, k3)]
            m = jnp.max(s[0], axis=1, keepdims=True)
            for i in range(1, 4):
                m = jnp.where(allow[i] == 1, jnp.maximum(m, jnp.max(s[i], axis=1, keepdims=True)), m)
            p = [jnp.exp2((s[0] - m) * C)] + [jnp.exp2((s[i] - m) * (C * on[i])) for i in range(1, 4)]
            total = jnp.sum(p[0], axis=1, keepdims=True)
            for i in range(1, 4):
                total += on[i] * jnp.sum(p[i], axis=1, keepdims=True)
            inverse = 1.0 / total
            acc = jnp.dot(p[0].astype(BF16), v0[:, hs], preferred_element_type=F32)
            for i, v in ((1, v1), (2, v2)):
                acc += on[i] * jnp.dot(p[i].astype(BF16), v[:, hs], preferred_element_type=F32)
            acc_ref[cs, hs] = acc * inverse
            p_ref[h, cs, :] = (p[3] * (inverse * on[3])).astype(BF16)


def attend_last(acc_ref, p_ref, v3, o_ref):
    for h in range(v3.shape[1] // HD):
        hs = pl.ds(h * HD, HD)
        o_ref[:, hs] = (acc_ref[:, hs] + jnp.dot(p_ref[h], v3[:, hs], preferred_element_type=F32)).astype(BF16)


def kernel_call(body, ints, args, outs, name, flops, exps=0, space=24):
    moved = sum(a.size * a.dtype.itemsize for a in (*args, *outs))
    return pl.pallas_call(
        body,
        in_specs=[SCALARS] * len(ints) + [ON_CHIP] * len(args),
        out_specs=[ON_CHIP] * len(outs),
        out_shape=outs,
        compiler_params=pltpu.CompilerParams(vmem_limit_bytes=space * 2**20),
        cost_estimate=pl.CostEstimate(flops=flops, transcendentals=exps, bytes_accessed=moved),
        name=name,
    )(*ints, *args)


def project_near(a0, a1, w0, w1, t):
    t[...] = jnp.dot(a0[...], w0[...], preferred_element_type=F32)
    t[...] += jnp.dot(a1[...], w1[...], preferred_element_type=F32)


def project_far(ints, t, a2, a3, w2, w3, gate, columns):
    k = a2.shape[1]
    swapped = ints[1] == 1
    x2 = jnp.where(swapped, a3[...], a2[...])
    x3 = jnp.where(swapped, a2[...], a3[...])
    total = t[:, columns] + jnp.dot(x2, w2[:, columns], preferred_element_type=F32)
    total += jnp.dot(x3, w3[:, columns], preferred_element_type=F32)
    return gate[pl.ds(ints[0], 1), columns] * total


def project_velocity(ints, t, a2, a3, w2, w3, gate, out):
    for j in range(out.shape[1] // CHUNK):
        columns = pl.ds(j * CHUNK, CHUNK)
        out[:, columns] = project_far(ints, t, a2, a3, w2, w3, gate, columns).astype(BF16)


def project_next(ints, delta, t, a2, a3, w2, w3, gate, lat_a, lat_b, fresh, out):
    half = lat_a.shape[0]
    for j in range(out.shape[1] // CHUNK):
        columns = pl.ds(j * CHUNK, CHUNK)
        update = delta[0] * project_far(ints, t, a2, a3, w2, w3, gate, columns)
        for i, lat in enumerate((lat_a, lat_b)):
            rows = pl.ds(i * half, half)
            new = (lat[:, columns].astype(F32) + update[i * half : (i + 1) * half]).astype(BF16)
            out[rows, columns] = jnp.where(ints[2] == 1, fresh[rows, columns], new)


def both(pairs_of):
    pairs = []
    for place in np.ndindex(NY, NXL, NZ, 2, 2):
        (y, x_lo, z, x_hi, core), (y2, x_lo2, z2, x_hi2, core2) = place, pairs_of(*place)
        number = lambda y, x_lo, z, x_hi, core: ((y * NXL + x_lo) * NZ + z) * 4 + x_hi * 2 + core
        pairs.append((number(*place), number(y2, x_lo2, z2, x_hi2, core2)))
    return pairs


def across(value):
    pairs = both(lambda y, x_lo, z, x_hi, core: (y, 1 - x_lo, z, 1 - x_hi, core ^ (y % 2)))
    return lax.ppermute(value, ("frame", "head"), pairs)


def shards(latents, queries, keys, values, out_weight, gate_table, levels, block_mask, fresh):
    frame = lax.axis_index("frame")
    head = lax.axis_index("head")
    spans = lax.axis_size("frame")
    window = block_mask.shape[1]
    rows, width = latents.shape
    rows_w = out_weight.shape[0]
    heads = queries.shape[1] // HD
    barrier = lax.optimization_barrier

    odd = (frame // (NXL * NZ)) % 2
    core = head % 2
    other = (1 - head // 2) * 2 + (core ^ odd)
    columns_of = lambda weight, at: lax.dynamic_slice(weight, (0, at * width), (rows_w, width))

    k_r1 = ring(keys, 1)
    q_next = ring(queries, -1)
    v_r1 = ring(values, 1)
    k_l1 = ring(keys, -1)
    w_far = across(columns_of(out_weight, other))
    meta = jnp.concatenate([block_mask[0], levels])
    k_r1, v_r1, q_next, k_l1, values_, lat_a, lat_b, meta = barrier(
        (k_r1, v_r1, q_next, k_l1, values, latents[: rows // 2], latents[rows // 2 :], meta)
    )

    k_r2 = ring(k_r1, 1)
    v_l1 = ring(values_, -1)
    v_r2 = ring(v_r1, 1)
    lat_a = ring(lat_a, -1)
    meta_next = ring(meta, -1)
    w_far2 = lax.ppermute(
        w_far, "frame", [(i, (((i // 16) ^ 1) * 16) + i % 16) for i in range(NY * NXL * NZ)]
    )

    span = lax.rem(frame + 1, spans)
    distances = jnp.arange(window, dtype=jnp.int32)
    allow = ((meta_next[:window] == 1) & (span - distances >= 0)).astype(jnp.int32)
    work = heads * rows * rows
    half = jax.ShapeDtypeStruct((rows, heads * HD), F32)
    acc, p3 = kernel_call(
        attend_first,
        (allow,),
        (q_next, k_l1, v_l1, keys, values, k_r1, v_r1, k_r2),
        (half, jax.ShapeDtypeStruct((heads, rows, rows), BF16)),
        "attend_first",
        14 * work * HD,
        4 * work,
    )
    v_r2, lat_a, lat_b, out_weight_ = barrier((v_r2, lat_a, lat_b, out_weight))
    (attended,) = kernel_call(
        attend_last,
        (),
        (acc, p3, v_r2),
        (jax.ShapeDtypeStruct((rows, heads * HD), BF16),),
        "attend_last",
        2 * work * HD,
    )

    mine = ring(attended, 1)
    partner1 = swap(attended, PARTNER)
    sibling1 = swap(attended, SIBLING)
    lat_b = ring(lat_b, -1)
    w_own = columns_of(out_weight_, head)
    w_sib = swap(columns_of(out_weight_, head ^ 1), SIBLING)
    near = jax.ShapeDtypeStruct((rows, width), F32)
    flops = 4 * rows * width * heads * HD
    (t1,) = kernel_call(project_near, (), (attended, sibling1, w_own, w_sib), (near,), "near_next", flops)
    partner1, mine, sibling1, w_sib = barrier((partner1, mine, sibling1, w_sib))
    partner2 = swap(mine, PARTNER)
    other1 = swap(partner1, SIBLING)
    sibling2 = swap(mine, SIBLING)

    def scalars(level):
        at = level.astype(F32)
        delta = noise_level(at / LEVELS) - noise_level((at + 1.0) / LEVELS)
        is_last = (frame == spans - 1).astype(jnp.int32)
        return jnp.stack([level, odd, is_last]), delta[None]

    out = jax.ShapeDtypeStruct((rows, width), BF16)
    ints, delta = scalars(meta_next[window])
    (next_latents,) = kernel_call(
        project_next,
        (ints, delta),
        (t1, partner1, other1, w_far, w_far2, gate_table, lat_a, lat_b, fresh),
        (out,),
        "project_next",
        flops,
    )
    (t2,) = kernel_call(project_near, (), (mine, sibling2, w_own, w_sib), (near,), "near_velocity", flops)
    partner2, next_latents, t2 = barrier((partner2, next_latents, t2))
    ints, _ = scalars(levels[0])
    (velocity,) = kernel_call(
        project_velocity,
        (ints,),
        (t2, partner2, swap(partner2, SIBLING), w_far, w_far2, gate_table),
        (out,),
        "project_velocity",
        flops,
    )
    return velocity, next_latents


def solution(mesh):
    in_specs = (
        P("frame", "head"),
        P("frame", "head"),
        P("frame", "head"),
        P("frame", "head"),
        P("head", None),
        P(None, "head"),
        P("frame"),
        P("frame", None),
        P(None, "head"),
    )
    out_specs = (P("frame", "head"), P("frame", "head"))
    return jax.shard_map(shards, mesh=mesh, in_specs=in_specs, out_specs=out_specs, check_vma=False)
```

time: 224 us -> 167 us (0.75)
  waiting for transfers between devices: 144 us -> 80.5 us
  Pallas kernels: 0 us -> 27.7 us
  matrix products: 22.8 us -> 0 us
  other arithmetic: 11.5 us -> 1.52 us
  starting transfers between devices: 24.3 us -> 32.6 us
  local copies, waits for them, and re-layouts: 17.4 us -> 20.5 us
    all_to_all x1 -> x0, waiting for transfers between devices: 59.1 us -> none  [sent_and_summed(): lax.all_to_all(tiles, axis, split_axis=0, concat_axis=0, tiled=True)]
    pallas_call x0 -> x6, Pallas kernels: none -> 27.7 us  [kernel_call(): pl.pallas_call(body, in_specs=[SCALARS] * len(ints) + [ON_CHIP] * len(arg...]
    dot_general x4 -> x0, matrix products: 22.8 us -> none  [the longest x1 10.7 us: shards(): jnp.einsum('hqbk,bkhd->qhd', weights, value_heads, preferred_element_type...]
    ppermute x7 -> x20, starting transfers between devices: 18.1 us -> 32.6 us  [the longest x11 17.7 us: ring(): return lax.ppermute(value, 'frame', [(i, (i + by) % n) for i in range(n)])]
    reduce_sum x2 -> x0, other arithmetic: 8.27 us -> none  [the longest x1 4.67 us: shards(): jnp.sum(expd, axis=(2, 3), keepdims=True)]
    all_to_all x1 -> x0, starting transfers between devices: 6.24 us -> none  [sent_and_summed(): lax.all_to_all(tiles, axis, split_axis=0, concat_axis=0, tiled=True)]
    dynamic_slice x0 -> x2, local copies, waits for them, and re-layouts: none -> 6.03 us  [shards(): lax.dynamic_slice(weight, (0, at * width), (rows_w, width))]
    ppermute x7 -> x20, waiting for transfers between devices: 85.2 us -> 80.5 us  [the longest x11 62.8 us: ring(): return lax.ppermute(value, 'frame', [(i, (i + by) % n) for i in range(n)])]
  transfers between devices with their start and end apart: 8 -> 20, of which waited for: 8 -> 9; matrix products, arithmetic and copies ran while one was open for 9% -> 6% of each run, Pallas kernels for 0% -> 13%
where the time goes in v1:
time: 167 us; the launch traced here: 165 us
  waiting for transfers between devices  80.5 us (48%)
  starting transfers between devices  32.6 us (20%)
  Pallas kernels  27.7 us (17%)
  local copies, waits for them, and re-layouts  20.5 us (12%)
  between operations  2.16 us (1%)
    ppermute x11, waiting for transfers between devices, ring(): return lax.ppermute(value, 'frame', [(i, (i + by) % n) for i in range(n)])  62.8 us
    pallas_call x6, Pallas kernels, kernel_call(): pl.pallas_call(body, in_specs=[SCALARS] * len(ints) + [ON_CHIP] * len(arg...  27.7 us
    ppermute x11, starting transfers between devices, ring(): return lax.ppermute(value, 'frame', [(i, (i + by) % n) for i in range(n)])  17.7 us
    ppermute x7, waiting for transfers between devices, swap(): return lax.ppermute(value, 'head', pairs)  15.4 us
    unnamed x34, local copies, waits for them, and re-layouts  11.6 us
    ppermute x7, starting transfers between devices, swap(): return lax.ppermute(value, 'head', pairs)  8.94 us
    dynamic_slice x2, local copies, waits for them, and re-layouts, shards(): lax.dynamic_slice(weight, (0, at * width), (rows_w, width))  6.03 us
  transfers between devices with their start and end apart: 20, of which 9 were waited for; matrix products, arithmetic and copies ran while one was open for 6% of the time, Pallas kernels for 13%

profile of v1, /device:TPU:9, one launch (start us, length us, event | category | flops | bytes accessed | tf_op | source)
XLA Modules:
  0.0 164.9 jit_solution(9754217670902118271)
XLA Ops:
  4.0 3.3 %collective-permute-start.2 = (bf16[512,640]{1,0:T(8,128)(2,1)}, bf16[512,640]{1,0:T(8,128)(2,1)S(1)}, u32[]{:S(2)}, u32[]{:S(2)}) collective-permute-start(bf16[512,640]{1,0:T(8,128)(2,1)} %param.10), channel_id=1, source_target_pairs={{0,252},{4,0},{8,4},{12,8},{16,12},{20,16},{24,20},{28,24},{32,28}... | collective-permute-start | bytes 1966088 | tf_op jit(solution)/shard_map/ppermute | solution.py:28
  10.1 2.2 %fusion = (bf16[256,1280]{1,0:T(8,128)(2,1)}, bf16[256,1280]{1,0:T(8,128)(2,1)S(1)}) fusion(bf16[512,1280]{1,0:T(8,128)(2,1)} %param.9), kind=kLoop, calls=%fused_computation.7 | loop fusion | bytes 2621440 | tf_op jit(solution)/shard_map/slice | solution.py:152
  12.3 9.6 %collective-permute-done.k2 = bf16[512,640]{1,0:T(8,128)(2,1)} collective-permute-done((bf16[512,640]{1,0:T(8,128)(2,1)}, bf16[512,640]{1,0:T(8,128)(2,1)}, u32[]{:S(2)}, u32[]{:S(2)}) %collective-permute-start) | collective-permute-done | bytes 655392 | tf_op jit(solution)/shard_map/ppermute | solution.py:28
  21.9 13.9 %collective-permute-done.1.v2 = bf16[512,640]{1,0:T(8,128)(2,1)S(1)} collective-permute-done((bf16[512,640]{1,0:T(8,128)(2,1)}, bf16[512,640]{1,0:T(8,128)(2,1)S(1)}, u32[]{:S(2)}, u32[]{:S(2)}) %collective-permute-start.1) | collective-permute-done | bytes 655392 | tf_op jit(solution)/shard_map/ppermute | solution.py:28
  37.5 4.5 %collective-permute-start.8 = (bf16[256,1280]{1,0:T(8,128)(2,1)S(1)}, bf16[256,1280]{1,0:T(8,128)(2,1)S(1)}, u32[]{:S(2)}, u32[]{:S(2)}) collective-permute-start(bf16[256,1280]{1,0:T(8,128)(2,1)S(1)} %get-tuple-element.30), channel_id=1, source_target_pairs={{0,252},{4,0},{8,4},{12,8},{16,12},{20,16},{24,20},{28,24},{32,28}... | collective-permute-start | bytes 1966088 | tf_op jit(solution)/shard_map/ppermute | solution.py:28
  42.0 2.7 %constant_dynamic-slice_fusion = bf16[640,1280]{1,0:T(8,128)(2,1)} fusion(bf16[640,5120]{1,0:T(8,128)(2,1)} %param.13, s32[]{:T(128)S(6)} %select_n.33), kind=kLoop, calls=%fused_computation.1 | loop fusion | bytes 3276804 | tf_op jit(solution)/shard_map/dynamic_slice | solution.py:143
  44.7 2.7 %collective-permute-start.15 = (bf16[640,1280]{1,0:T(8,128)(2,1)}, bf16[640,1280]{1,0:T(8,128)(2,1)}, u32[]{:S(2)}, u32[]{:S(2)}) collective-permute-start(bf16[640,1280]{1,0:T(8,128)(2,1)} %constant_dynamic-slice_fusion), channel_id=1, source_target_pairs={{0,34},{1,35},{2,32},{3,33},{4,38},{5,39},{6,36},{7,37},{8,42},{9,... | collective-permute-start | bytes 4915208 | tf_op jit(solution)/shard_map/ppermute | solution.py:127
  47.4 8.1 %collective-permute-done.7.v3 = bf16[512,640]{1,0:T(8,128)(2,1)S(1)} collective-permute-done((bf16[512,640]{1,0:T(8,128)(2,1)S(1)}, bf16[512,640]{1,0:T(8,128)(2,1)S(1)}, u32[]{:S(2)}, u32[]{:S(2)}) %collective-permute-start.7) | collective-permute-done | bytes 655392 | tf_op jit(solution)/shard_map/ppermute | solution.py:28
  57.2 3.3 %constant_dynamic-slice_fusion.1 = (bf16[640,1280]{1,0:T(8,128)(2,1)S(1)}, bf16[640,1280]{1,0:T(8,128)(2,1)}) fusion(bf16[640,5120]{1,0:T(8,128)(2,1)} %param.13, s32[]{:T(128)S(6)} %select_n.30, s32[]{:T(128)S(6)} %select_n.29), kind=kLoop, calls=%fused_computation.2 | loop fusion | bytes 6553608 | tf_op jit(solution)/shard_map/dynamic_slice | solution.py:143
  60.5 2.2 %collective-permute-start.12 = (bf16[640,1280]{1,0:T(8,128)(2,1)}, bf16[640,1280]{1,0:T(8,128)(2,1)S(1)}, u32[]{:S(2)}, u32[]{:S(2)}) collective-permute-start(bf16[640,1280]{1,0:T(8,128)(2,1)} %get-tuple-element.43), channel_id=1, source_target_pairs={{0,1},{1,0},{2,3},{3,2},{4,5},{5,4},{6,7},{7,6},{8,9},{9,8},{10,11... | collective-permute-start | bytes 4915208 | tf_op jit(solution)/shard_map/ppermute | solution.py:32
  62.7 4.5 %collective-permute-start.5 = (bf16[512,640]{1,0:T(8,128)(2,1)}, bf16[512,640]{1,0:T(8,128)(2,1)}, u32[]{:S(2)}, u32[]{:S(2)}) collective-permute-start(bf16[512,640]{1,0:T(8,128)(2,1)} %v1.1), channel_id=1, source_target_pairs={{0,252},{4,0},{8,4},{12,8},{16,12},{20,16},{24,20},{28,24},{32,28}... | collective-permute-start | bytes 1966088 | tf_op jit(solution)/shard_map/ppermute | solution.py:28
  67.8 13.5 %collective-permute-done.4 = s32[5]{0:T(128)S(1)} collective-permute-done((s32[5]{0:T(128)S(1)}, s32[5]{0:T(128)S(1)}, u32[]{:S(2)}, u32[]{:S(2)}) %collective-permute-start.4) | collective-permute-done | bytes 52 | tf_op jit(solution)/shard_map/ppermute | solution.py:28
  81.3 2.2 %collective-permute-done.15.w2 = bf16[640,1280]{1,0:T(8,128)(2,1)} collective-permute-done((bf16[640,1280]{1,0:T(8,128)(2,1)}, bf16[640,1280]{1,0:T(8,128)(2,1)}, u32[]{:S(2)}, u32[]{:S(2)}) %collective-permute-start.15) | collective-permute-done | bytes 1638432 | tf_op jit(solution)/shard_map/ppermute | solution.py:127
  83.5 3.2 %collective-permute-start.16 = (bf16[640,1280]{1,0:T(8,128)(2,1)}, bf16[640,1280]{1,0:T(8,128)(2,1)}, u32[]{:S(2)}, u32[]{:S(2)}) collective-permute-start(bf16[640,1280]{1,0:T(8,128)(2,1)} %collective-permute-done.15.w2), channel_id=1, source_target_pairs={{0,64},{4,68},{8,72},{12,76},{16,80},{20,84},{24,88},{28,92},{32,9... | collective-permute-start | bytes 4915208 | tf_op jit(solution)/shard_map/ppermute | solution.py:160
  91.1 9.6 %attend_first.1 = (f32[512,640]{1,0:T(8,128)S(1)}, bf16[5,512,512]{2,1,0:T(8,128)(2,1)S(1)}) custom-call(s32[4]{0:T(128)S(1)} %and_convert_fusion.allow, bf16[512,640]{1,0:T(8,128)(2,1)S(1)} %copy-done.14, bf16[512,640]{1,0:T(8,128)(2,1)S(1)} %copy-done.16, bf16[512,640]{1,0:T(8,128)(2,1)} %collective-permute-done.5.v0, bf16[512,640]{1,0:T(8,128)(2,1)S(1)} %copy-done.10, ...), custom_call_target="tpu_custom_call" | custom-call | flops 2348810240 | bytes 9175040 | tf_op jit(solution)/shard_map/attend_first/pallas_call | solution.py:73
  101.7 2.0 %collective-permute-start.11 = (bf16[512,640]{1,0:T(8,128)(2,1)S(1)}, bf16[512,640]{1,0:T(8,128)(2,1)S(1)}, u32[]{:S(2)}, u32[]{:S(2)}) collective-permute-start(bf16[512,640]{1,0:T(8,128)(2,1)S(1)} %attend_last.1.a0), channel_id=1, source_target_pairs={{0,1},{1,0},{2,3},{3,2},{4,5},{5,4},{6,7},{7,6},{8,9},{9,8},{10,11... | collective-permute-start | bytes 1966088 | tf_op jit(solution)/shard_map/ppermute | solution.py:32
  103.7 1.9 %collective-permute-start.9 = (bf16[512,640]{1,0:T(8,128)(2,1)S(1)}, bf16[512,640]{1,0:T(8,128)(2,1)}, u32[]{:S(2)}, u32[]{:S(2)}) collective-permute-start(bf16[512,640]{1,0:T(8,128)(2,1)S(1)} %attend_last.1.a0), channel_id=1, source_target_pairs={{0,2},{2,0},{1,3},{3,1},{4,6},{6,4},{5,7},{7,5},{8,10},{10,8},{9,1... | collective-permute-start | bytes 1966088 | tf_op jit(solution)/shard_map/ppermute | solution.py:32
  106.5 12.7 %collective-permute-done.10.a0 = bf16[512,640]{1,0:T(8,128)(2,1)} collective-permute-done((bf16[512,640]{1,0:T(8,128)(2,1)S(1)}, bf16[512,640]{1,0:T(8,128)(2,1)}, u32[]{:S(2)}, u32[]{:S(2)}) %collective-permute-start.10) | collective-permute-done | bytes 655392 | tf_op jit(solution)/shard_map/ppermute | solution.py:28
  120.0 13.6 %collective-permute-done.9.a2 = bf16[512,640]{1,0:T(8,128)(2,1)} collective-permute-done((bf16[512,640]{1,0:T(8,128)(2,1)S(1)}, bf16[512,640]{1,0:T(8,128)(2,1)}, u32[]{:S(2)}, u32[]{:S(2)}) %collective-permute-start.9) | collective-permute-done | bytes 655392 | tf_op jit(solution)/shard_map/ppermute | solution.py:32
  139.9 2.2 %near_next.1.t = f32[512,1280]{1,0:T(8,128)S(1)} custom-call(bf16[512,640]{1,0:T(8,128)(2,1)S(1)} %copy-done.1, bf16[512,640]{1,0:T(8,128)(2,1)S(1)} %copy-done.6, bf16[640,1280]{1,0:T(8,128)(2,1)S(1)} %get-tuple-element.42.w0, bf16[640,1280]{1,0:T(8,128)(2,1)S(1)} %collective-permute-done.12.w1), custom_call_target="tpu_custom_call" | custom-call | flops 1677721600 | bytes 7208960 | tf_op jit(solution)/shard_map/near_next/pallas_call | solution.py:73
  142.1 3.6 %near_velocity.1.t = f32[512,1280]{1,0:T(8,128)S(1)} custom-call(bf16[512,640]{1,0:T(8,128)(2,1)} %collective-permute-done.10.a0, bf16[512,640]{1,0:T(8,128)(2,1)} %collective-permute-done.18.a1, bf16[640,1280]{1,0:T(8,128)(2,1)S(1)} %get-tuple-element.42.w0, bf16[640,1280]{1,0:T(8,128)(2,1)S(1)} %collective-permute-done.12.w1), custom_call_target="tpu_custom_call" | custom-call | flops 1677721600 | bytes 7208960 | tf_op jit(solution)/shard_map/near_velocity/pallas_call | solution.py:73
  145.8 4.9 %collective-permute-done.17.lat_b = bf16[256,1280]{1,0:T(8,128)(2,1)} collective-permute-done((bf16[256,1280]{1,0:T(8,128)(2,1)}, bf16[256,1280]{1,0:T(8,128)(2,1)}, u32[]{:S(2)}, u32[]{:S(2)}) %collective-permute-start.17) | collective-permute-done | bytes 655392 | tf_op jit(solution)/shard_map/ppermute | solution.py:28
  150.7 5.9 %project_next.1 = bf16[512,1280]{1,0:T(8,128)(2,1)} custom-call(s32[3]{0:T(128)S(1)} %add_add_fusion.1.ints, f32[1]{0:T(128)S(6)} %sub.25.delta, f32[512,1280]{1,0:T(8,128)S(1)} %near_next.1.t, bf16[512,640]{1,0:T(8,128)(2,1)} %collective-permute-done.9.a2, bf16[512,640]{1,0:T(8,128)(2,1)} %collective-permute-done.14.a3, ...), custom_call_target="tpu_custom_call" | custom-call | flops 1677721600 | bytes 11161600 | tf_op jit(solution)/shard_map/project_next/pallas_call | solution.py:73
  159.4 5.5 %project_velocity.1 = bf16[512,1280]{1,0:T(8,128)(2,1)} custom-call(s32[3]{0:T(128)S(1)} %add_add_fusion.ints, f32[512,1280]{1,0:T(8,128)S(1)} %near_velocity.1.t, bf16[512,640]{1,0:T(8,128)(2,1)} %collective-permute-done.13.a2, bf16[512,640]{1,0:T(8,128)(2,1)S(1)} %collective-permute-done.19.a3, bf16[640,1280]{1,0:T(8,128)(2,1)} %collective-permute-done.15.w2, ...), custom_call_target="tpu_custom_call" | custom-call | flops 1677721600 | bytes 8540160 | tf_op jit(solution)/shard_map/project_velocity/pallas_call | solution.py:73
  (64 shorter events, 24.8 us)
Async XLA Ops:
  0.6 21.2 %collective-permute-start = (bf16[512,640]{1,0:T(8,128)(2,1)}, bf16[512,640]{1,0:T(8,128)(2,1)}, u32[]{:S(2)}, u32[]{:S(2)}) collective-permute-start(bf16[512,640]{1,0:T(8,128)(2,1)} %k1.1), channel_id=1, source_target_pairs={{0,4},{4,8},{8,12},{12,16},{16,20},{20,24},{24,28},{28,32},{32,36}... | collective-permute-start | bytes 1966088 | tf_op jit(solution)/shard_map/ppermute | solution.py:28
  2.3 33.5 %collective-permute-start.1 = (bf16[512,640]{1,0:T(8,128)(2,1)}, bf16[512,640]{1,0:T(8,128)(2,1)S(1)}, u32[]{:S(2)}, u32[]{:S(2)}) collective-permute-start(bf16[512,640]{1,0:T(8,128)(2,1)} %v1.1), channel_id=1, source_target_pairs={{0,4},{4,8},{8,12},{12,16},{16,20},{20,24},{24,28},{28,32},{32,36}... | collective-permute-start | bytes 1966088 | tf_op jit(solution)/shard_map/ppermute | solution.py:28
  4.0 31.8 %collective-permute-start.2 = (bf16[512,640]{1,0:T(8,128)(2,1)}, bf16[512,640]{1,0:T(8,128)(2,1)S(1)}, u32[]{:S(2)}, u32[]{:S(2)}) collective-permute-start(bf16[512,640]{1,0:T(8,128)(2,1)} %param.10), channel_id=1, source_target_pairs={{0,252},{4,0},{8,4},{12,8},{16,12},{20,16},{24,20},{28,24},{32,28}... | collective-permute-start | bytes 1966088 | tf_op jit(solution)/shard_map/ppermute | solution.py:28
  7.3 29.4 %collective-permute-start.3 = (bf16[512,640]{1,0:T(8,128)(2,1)}, bf16[512,640]{1,0:T(8,128)(2,1)S(1)}, u32[]{:S(2)}, u32[]{:S(2)}) collective-permute-start(bf16[512,640]{1,0:T(8,128)(2,1)} %k1.1), channel_id=1, source_target_pairs={{0,252},{4,0},{8,4},{12,8},{16,12},{20,16},{24,20},{28,24},{32,28}... | collective-permute-start | bytes 1966088 | tf_op jit(solution)/shard_map/ppermute | solution.py:28
  35.8 8.9 %copy-start.11 = (bf16[512,640]{1,0:T(8,128)(2,1)}, bf16[512,640]{1,0:T(8,128)(2,1)S(1)}, u32[]{:S(2)}) copy-start(bf16[512,640]{1,0:T(8,128)(2,1)S(1)} %collective-permute-done.1.v2) | copy-start | bytes 1966084
  37.5 18.0 %collective-permute-start.7 = (bf16[512,640]{1,0:T(8,128)(2,1)S(1)}, bf16[512,640]{1,0:T(8,128)(2,1)S(1)}, u32[]{:S(2)}, u32[]{:S(2)}) collective-permute-start(bf16[512,640]{1,0:T(8,128)(2,1)S(1)} %collective-permute-done.1.v2), channel_id=1, source_target_pairs={{0,4},{4,8},{8,12},{12,16},{16,20},{20,24},{24,28},{28,32},{32,36}... | collective-permute-start | bytes 1966088 | tf_op jit(solution)/shard_map/ppermute | solution.py:28
  37.5 18.8 %collective-permute-start.8 = (bf16[256,1280]{1,0:T(8,128)(2,1)S(1)}, bf16[256,1280]{1,0:T(8,128)(2,1)S(1)}, u32[]{:S(2)}, u32[]{:S(2)}) collective-permute-start(bf16[256,1280]{1,0:T(8,128)(2,1)S(1)} %get-tuple-element.30), channel_id=1, source_target_pairs={{0,252},{4,0},{8,4},{12,8},{16,12},{20,16},{24,20},{28,24},{32,28}... | collective-permute-start | bytes 1966088 | tf_op jit(solution)/shard_map/ppermute | solution.py:28
  44.7 38.8 %collective-permute-start.15 = (bf16[640,1280]{1,0:T(8,128)(2,1)}, bf16[640,1280]{1,0:T(8,128)(2,1)}, u32[]{:S(2)}, u32[]{:S(2)}) collective-permute-start(bf16[640,1280]{1,0:T(8,128)(2,1)} %constant_dynamic-slice_fusion), channel_id=1, source_target_pairs={{0,34},{1,35},{2,32},{3,33},{4,38},{5,39},{6,36},{7,37},{8,42},{9,... | collective-permute-start | bytes 4915208 | tf_op jit(solution)/shard_map/ppermute | solution.py:127
  60.5 73.1 %collective-permute-start.12 = (bf16[640,1280]{1,0:T(8,128)(2,1)}, bf16[640,1280]{1,0:T(8,128)(2,1)S(1)}, u32[]{:S(2)}, u32[]{:S(2)}) collective-permute-start(bf16[640,1280]{1,0:T(8,128)(2,1)} %get-tuple-element.43), channel_id=1, source_target_pairs={{0,1},{1,0},{2,3},{3,2},{4,5},{5,4},{6,7},{7,6},{8,9},{9,8},{10,11... | collective-permute-start | bytes 4915208 | tf_op jit(solution)/shard_map/ppermute | solution.py:32
  62.7 24.1 %collective-permute-start.6 = (bf16[512,640]{1,0:T(8,128)(2,1)}, bf16[512,640]{1,0:T(8,128)(2,1)}, u32[]{:S(2)}, u32[]{:S(2)}) collective-permute-start(bf16[512,640]{1,0:T(8,128)(2,1)} %collective-permute-done.k2), channel_id=1, source_target_pairs={{0,4},{4,8},{8,12},{12,16},{16,20},{20,24},{24,28},{28,32},{32,36}... | collective-permute-start | bytes 1966088 | tf_op jit(solution)/shard_map/ppermute | solution.py:28
  62.7 24.1 %collective-permute-start.5 = (bf16[512,640]{1,0:T(8,128)(2,1)}, bf16[512,640]{1,0:T(8,128)(2,1)}, u32[]{:S(2)}, u32[]{:S(2)}) collective-permute-start(bf16[512,640]{1,0:T(8,128)(2,1)} %v1.1), channel_id=1, source_target_pairs={{0,252},{4,0},{8,4},{12,8},{16,12},{20,16},{24,20},{28,24},{32,28}... | collective-permute-start | bytes 1966088 | tf_op jit(solution)/shard_map/ppermute | solution.py:28
  67.2 14.2 %collective-permute-start.4 = (s32[5]{0:T(128)S(1)}, s32[5]{0:T(128)S(1)}, u32[]{:S(2)}, u32[]{:S(2)}) collective-permute-start(s32[5]{0:T(128)S(1)} %pad_add_fusion), channel_id=1, source_target_pairs={{0,252},{4,0},{8,4},{12,8},{16,12},{20,16},{24,20},{28,24},{32,28}... | collective-permute-start | bytes 68 | tf_op jit(solution)/shard_map/ppermute | solution.py:28
  81.3 19.4 %copy-start.4 = (bf16[512,640]{1,0:T(8,128)(2,1)S(1)}, bf16[512,640]{1,0:T(8,128)(2,1)}, u32[]{:S(2)}) copy-start(bf16[512,640]{1,0:T(8,128)(2,1)} %copy-done.3) | copy-start | bytes 1966084
  83.5 67.1 %collective-permute-start.16 = (bf16[640,1280]{1,0:T(8,128)(2,1)}, bf16[640,1280]{1,0:T(8,128)(2,1)}, u32[]{:S(2)}, u32[]{:S(2)}) collective-permute-start(bf16[640,1280]{1,0:T(8,128)(2,1)} %collective-permute-done.15.w2), channel_id=1, source_target_pairs={{0,64},{4,68},{8,72},{12,76},{16,80},{20,84},{24,88},{28,92},{32,9... | collective-permute-start | bytes 4915208 | tf_op jit(solution)/shard_map/ppermute | solution.py:160
  101.6 17.6 %collective-permute-start.10 = (bf16[512,640]{1,0:T(8,128)(2,1)S(1)}, bf16[512,640]{1,0:T(8,128)(2,1)}, u32[]{:S(2)}, u32[]{:S(2)}) collective-permute-start(bf16[512,640]{1,0:T(8,128)(2,1)S(1)} %attend_last.1.a0), channel_id=1, source_target_pairs={{0,4},{4,8},{8,12},{12,16},{16,20},{20,24},{24,28},{28,32},{32,36}... | collective-permute-start | bytes 1966088 | tf_op jit(solution)/shard_map/ppermute | solution.py:28
  101.7 17.5 %collective-permute-start.11 = (bf16[512,640]{1,0:T(8,128)(2,1)S(1)}, bf16[512,640]{1,0:T(8,128)(2,1)S(1)}, u32[]{:S(2)}, u32[]{:S(2)}) collective-permute-start(bf16[512,640]{1,0:T(8,128)(2,1)S(1)} %attend_last.1.a0), channel_id=1, source_target_pairs={{0,1},{1,0},{2,3},{3,2},{4,5},{5,4},{6,7},{7,6},{8,9},{9,8},{10,11... | collective-permute-start | bytes 1966088 | tf_op jit(solution)/shard_map/ppermute | solution.py:32
  103.7 29.9 %collective-permute-start.9 = (bf16[512,640]{1,0:T(8,128)(2,1)S(1)}, bf16[512,640]{1,0:T(8,128)(2,1)}, u32[]{:S(2)}, u32[]{:S(2)}) collective-permute-start(bf16[512,640]{1,0:T(8,128)(2,1)S(1)} %attend_last.1.a0), channel_id=1, source_target_pairs={{0,2},{2,0},{1,3},{3,1},{4,6},{6,4},{5,7},{7,5},{8,10},{10,8},{9,1... | collective-permute-start | bytes 1966088 | tf_op jit(solution)/shard_map/ppermute | solution.py:32
  133.6 8.5 %collective-permute-start.18 = (bf16[512,640]{1,0:T(8,128)(2,1)}, bf16[512,640]{1,0:T(8,128)(2,1)}, u32[]{:S(2)}, u32[]{:S(2)}) collective-permute-start(bf16[512,640]{1,0:T(8,128)(2,1)} %collective-permute-done.10.a0), channel_id=1, source_target_pairs={{0,1},{1,0},{2,3},{3,2},{4,5},{5,4},{6,7},{7,6},{8,9},{9,8},{10,11... | collective-permute-start | bytes 1966088 | tf_op jit(solution)/shard_map/ppermute | solution.py:32
  134.1 16.6 %collective-permute-start.17 = (bf16[256,1280]{1,0:T(8,128)(2,1)}, bf16[256,1280]{1,0:T(8,128)(2,1)}, u32[]{:S(2)}, u32[]{:S(2)}) collective-permute-start(bf16[256,1280]{1,0:T(8,128)(2,1)} %get-tuple-element.37), channel_id=1, source_target_pairs={{0,252},{4,0},{8,4},{12,8},{16,12},{20,16},{24,20},{28,24},{32,28}... | collective-permute-start | bytes 1966088 | tf_op jit(solution)/shard_map/ppermute | solution.py:28
  134.1 16.6 %collective-permute-start.14 = (bf16[512,640]{1,0:T(8,128)(2,1)}, bf16[512,640]{1,0:T(8,128)(2,1)}, u32[]{:S(2)}, u32[]{:S(2)}) collective-permute-start(bf16[512,640]{1,0:T(8,128)(2,1)} %collective-permute-done.9.a2), channel_id=1, source_target_pairs={{0,1},{1,0},{2,3},{3,2},{4,5},{5,4},{6,7},{7,6},{8,9},{9,8},{10,11... | collective-permute-start | bytes 1966088 | tf_op jit(solution)/shard_map/ppermute | solution.py:32
  134.4 22.2 %collective-permute-start.13 = (bf16[512,640]{1,0:T(8,128)(2,1)}, bf16[512,640]{1,0:T(8,128)(2,1)}, u32[]{:S(2)}, u32[]{:S(2)}) collective-permute-start(bf16[512,640]{1,0:T(8,128)(2,1)} %collective-permute-done.10.a0), channel_id=1, source_target_pairs={{0,2},{2,0},{1,3},{3,1},{4,6},{6,4},{5,7},{7,5},{8,10},{10,8},{9,1... | collective-permute-start | bytes 1966088 | tf_op jit(solution)/shard_map/ppermute | solution.py:32
  142.1 8.6 %copy-start.2 = (bf16[512,1280]{1,0:T(8,128)(2,1)S(1)}, bf16[512,1280]{1,0:T(8,128)(2,1)}, u32[]{:S(2)}) copy-start(bf16[512,1280]{1,0:T(8,128)(2,1)} %fresh.1) | copy-start | bytes 3932164
  142.1 8.6 %copy-start.8 = (bf16[256,1280]{1,0:T(8,128)(2,1)S(1)}, bf16[256,1280]{1,0:T(8,128)(2,1)}, u32[]{:S(2)}) copy-start(bf16[256,1280]{1,0:T(8,128)(2,1)} %copy-done.7) | copy-start | bytes 1966084
  156.6 2.8 %collective-permute-start.19 = (bf16[512,640]{1,0:T(8,128)(2,1)}, bf16[512,640]{1,0:T(8,128)(2,1)S(1)}, u32[]{:S(2)}, u32[]{:S(2)}) collective-permute-start(bf16[512,640]{1,0:T(8,128)(2,1)} %collective-permute-done.13.a2), channel_id=1, source_target_pairs={{0,1},{1,0},{2,3},{3,2},{4,5},{5,4},{6,7},{7,6},{8,9},{9,8},{10,11... | collective-permute-start | bytes 1966088 | tf_op jit(solution)/shard_map/ppermute | solution.py:32
  (13 other events, 20.2 us)

commit v2 on v1

--- a/solution.py
+++ b/solution.py
@@ -36,30 +36,59 @@
 ON_CHIP = pl.BlockSpec(memory_space=pltpu.VMEM)
 SCALARS = pl.BlockSpec(memory_space=pltpu.SMEM)
 CHUNK = 256
-
-
-def attend_first(allow, q_ref, k0, v0, k1, v1, k2, v2, k3, acc_ref, p_ref):
+META = 16
+
+
+def attend_own(meta, q_ref, k, v, o_ref):
     rows, width = q_ref.shape
+    for c in range(rows // CHUNK):
+        cs = pl.ds(c * CHUNK, CHUNK)
+        lane = lax.broadcasted_iota(jnp.int32, (CHUNK, HD), 1)
+        side = jnp.zeros((CHUNK, HD), F32)
+        for i in range(meta.shape[0]):
+            side = jnp.where(lane == META + i, meta[i].astype(F32), side)
+        for h in range(width // HD):
+            hs = pl.ds(h * HD, HD)
+            s = lax.dot_general(q_ref[cs, hs], k[:, hs], NT, preferred_element_type=F32)
+            m = jnp.max(s, axis=1, keepdims=True)
+            p = jnp.exp2((s - m) * C)
+            total = jnp.sum(p, axis=1, keepdims=True)
+            o = jnp.dot(p.astype(BF16), v[:, hs], preferred_element_type=F32)
+            o_ref[cs, hs] = (o * (1.0 / total)).astype(BF16)
+            rest = m * C + jnp.log2(total)
+            for i in range(3):
+                part = rest.astype(BF16).astype(F32)
+                side = jnp.where(lane == 3 * h + i, part, side)
+                rest = rest - part
+        o_ref[cs, pl.ds(width, HD)] = side.astype(BF16)
+
+
+def attend_first(allow, q_ref, own, k1, v1, k2, v2, k3, acc_ref, p_ref):
+    rows, width = k1.shape
     on = [jnp.where(allow[i] == 1, 1.0, 0.0) for i in range(4)]
+    lane = lax.broadcasted_iota(jnp.int32, (CHUNK, HD), 1)
     for h in range(width // HD):
         hs = pl.ds(h * HD, HD)
         for c in range(rows // CHUNK):
             cs = pl.ds(c * CHUNK, CHUNK)
             q = q_ref[cs, hs]
-            s = [lax.dot_general(q, k[:, hs], NT, preferred_element_type=F32) for k in (k0, k1, k2, k3)]
-            m = jnp.max(s[0], axis=1, keepdims=True)
-            for i in range(1, 4):
-                m = jnp.where(allow[i] == 1, jnp.maximum(m, jnp.max(s[i], axis=1, keepdims=True)), m)
-            p = [jnp.exp2((s[0] - m) * C)] + [jnp.exp2((s[i] - m) * (C * on[i])) for i in range(1, 4)]
-            total = jnp.sum(p[0], axis=1, keepdims=True)
-            for i in range(1, 4):
-                total += on[i] * jnp.sum(p[i], axis=1, keepdims=True)
+            side = own[cs, pl.ds(width, HD)].astype(F32)
+            top = jnp.sum(jnp.where(lane // 3 == h, side, 0.0), axis=1, keepdims=True)
+            s = [lax.dot_general(q, k[:, hs], NT, preferred_element_type=F32) for k in (k1, k2, k3)]
+            m = top
+            for i in range(3):
+                m = jnp.where(allow[i + 1] == 1, jnp.maximum(m, jnp.max(s[i], axis=1, keepdims=True) * C), m)
+            p = [jnp.exp2((s[i] * C - m) * on[i + 1]) for i in range(3)]
+            first = jnp.exp2(top - m)
+            total = first
+            for i in range(3):
+                total += on[i + 1] * jnp.sum(p[i], axis=1, keepdims=True)
             inverse = 1.0 / total
-            acc = jnp.dot(p[0].astype(BF16), v0[:, hs], preferred_element_type=F32)
-            for i, v in ((1, v1), (2, v2)):
-                acc += on[i] * jnp.dot(p[i].astype(BF16), v[:, hs], preferred_element_type=F32)
+            acc = first * own[cs, hs].astype(F32)
+            for i, v in ((0, v1), (1, v2)):
+                acc += on[i + 1] * jnp.dot(p[i].astype(BF16), v[:, hs], preferred_element_type=F32)
             acc_ref[cs, hs] = acc * inverse
-            p_ref[h, cs, :] = (p[3] * (inverse * on[3])).astype(BF16)
+            p_ref[h, cs, :] = (p[2] * (inverse * on[3])).astype(BF16)
 
 
 def attend_last(acc_ref, p_ref, v3, o_ref):
@@ -68,7 +97,7 @@
         o_ref[:, hs] = (acc_ref[:, hs] + jnp.dot(p_ref[h], v3[:, hs], preferred_element_type=F32)).astype(BF16)
 
 
-def kernel_call(body, ints, args, outs, name, flops, exps=0, space=24):
+def kernel_call(body, ints, args, outs, name, flops, exps=0, space=44):
     moved = sum(a.size * a.dtype.itemsize for a in (*args, *outs))
     return pl.pallas_call(
         body,
@@ -76,7 +105,7 @@
         out_specs=[ON_CHIP] * len(outs),
         out_shape=outs,
         compiler_params=pltpu.CompilerParams(vmem_limit_bytes=space * 2**20),
-        cost_estimate=pl.CostEstimate(flops=flops, transcendentals=exps, bytes_accessed=moved),
+        cost_estimate=pl.CostEstimate(flops=1, transcendentals=0, bytes_accessed=1),
         name=name,
     )(*ints, *args)
 
@@ -142,40 +171,50 @@
     other = (1 - head // 2) * 2 + (core ^ odd)
     columns_of = lambda weight, at: lax.dynamic_slice(weight, (0, at * width), (rows_w, width))
 
+    work = heads * rows * rows
     k_r1 = ring(keys, 1)
+    v_r1 = ring(values, 1)
     q_next = ring(queries, -1)
-    v_r1 = ring(values, 1)
-    k_l1 = ring(keys, -1)
+    lat_a = ring(latents[: rows // 2], -1)
     w_far = across(columns_of(out_weight, other))
-    meta = jnp.concatenate([block_mask[0], levels])
-    k_r1, v_r1, q_next, k_l1, values_, lat_a, lat_b, meta = barrier(
-        (k_r1, v_r1, q_next, k_l1, values, latents[: rows // 2], latents[rows // 2 :], meta)
-    )
+    (own,) = kernel_call(
+        attend_own,
+        (jnp.concatenate([block_mask[0], levels]),),
+        (queries, keys, values),
+        (jax.ShapeDtypeStruct((rows, heads * HD + HD), BF16),),
+        "attend_own",
+        4 * work * HD,
+        work,
+    )
+    k_r1, v_r1, q_next, lat_a, own = barrier((k_r1, v_r1, q_next, lat_a, own))
 
     k_r2 = ring(k_r1, 1)
-    v_l1 = ring(values_, -1)
     v_r2 = ring(v_r1, 1)
-    lat_a = ring(lat_a, -1)
-    meta_next = ring(meta, -1)
+    own = ring(own, -1)
+    own, w_far, lat_b, out_weight_ = barrier((own, w_far, latents[rows // 2 :], out_weight))
+    lat_b = ring(lat_b, -1)
     w_far2 = lax.ppermute(
         w_far, "frame", [(i, (((i // 16) ^ 1) * 16) + i % 16) for i in range(NY * NXL * NZ)]
     )
+    at = heads * HD + META
+    meta_next = own[0, at : at + window + 1].astype(jnp.int32)
+    w_own = columns_of(out_weight_, head)
+    w_sib = columns_of(out_weight_, head ^ 1)
 
     span = lax.rem(frame + 1, spans)
     distances = jnp.arange(window, dtype=jnp.int32)
     allow = ((meta_next[:window] == 1) & (span - distances >= 0)).astype(jnp.int32)
-    work = heads * rows * rows
     half = jax.ShapeDtypeStruct((rows, heads * HD), F32)
     acc, p3 = kernel_call(
         attend_first,
         (allow,),
-        (q_next, k_l1, v_l1, keys, values, k_r1, v_r1, k_r2),
+        (q_next, own, keys, values, k_r1, v_r1, k_r2),
         (half, jax.ShapeDtypeStruct((heads, rows, rows), BF16)),
         "attend_first",
-        14 * work * HD,
-        4 * work,
-    )
-    v_r2, lat_a, lat_b, out_weight_ = barrier((v_r2, lat_a, lat_b, out_weight))
+        10 * work * HD,
+        3 * work,
+    )
+    v_r2, lat_b = barrier((v_r2, lat_b))
     (attended,) = kernel_call(
         attend_last,
         (),
@@ -185,16 +224,15 @@
         2 * work * HD,
     )
 
+    attended, w_own, w_sib = barrier((attended, w_own, w_sib))
     mine = ring(attended, 1)
     partner1 = swap(attended, PARTNER)
     sibling1 = swap(attended, SIBLING)
-    lat_b = ring(lat_b, -1)
-    w_own = columns_of(out_weight_, head)
-    w_sib = swap(columns_of(out_weight_, head ^ 1), SIBLING)
+    w_sib = swap(w_sib, SIBLING)
     near = jax.ShapeDtypeStruct((rows, width), F32)
     flops = 4 * rows * width * heads * HD
-    (t1,) = kernel_call(project_near, (), (attended, sibling1, w_own, w_sib), (near,), "near_next", flops)
-    partner1, mine, sibling1, w_sib = barrier((partner1, mine, sibling1, w_sib))
+    (t1,) = kernel_call(project_near, (), (attended, sibling1, w_own, w_sib), (near,), "near_next", flops, space=24)
+    partner1, mine, t1 = barrier((partner1, mine, t1))
     partner2 = swap(mine, PARTNER)
     other1 = swap(partner1, SIBLING)
     sibling2 = swap(mine, SIBLING)
@@ -214,9 +252,10 @@
         (out,),
         "project_next",
         flops,
-    )
-    (t2,) = kernel_call(project_near, (), (mine, sibling2, w_own, w_sib), (near,), "near_velocity", flops)
-    partner2, next_latents, t2 = barrier((partner2, next_latents, t2))
+        space=24,
+    )
+    (t2,) = kernel_call(project_near, (), (mine, sibling2, w_own, w_sib), (near,), "near_velocity", flops, space=24)
+    partner2, t2 = barrier((partner2, t2))
     ints, _ = scalars(levels[0])
     (velocity,) = kernel_call(
         project_velocity,
@@ -225,6 +264,7 @@
         (out,),
         "project_velocity",
         flops,
+        space=24,
     )
     return velocity, next_latents
 

time: 167 us -> 149 us (0.89); the launches traced: 165 us -> 149 us
  waiting for transfers between devices: 80.5 us -> 72.5 us
  local copies, waits for them, and re-layouts: 20.5 us -> 13.5 us
    ppermute x11 -> x9, waiting for transfers between devices: 62.8 us -> 44.7 us  [ring(): return lax.ppermute(value, 'frame', [(i, (i + by) % n) for i in range(n)])]
    ppermute x7, waiting for transfers between devices: 15.4 us -> 25.8 us  [swap(): return lax.ppermute(value, 'head', pairs)]
    unnamed x34 -> x30, local copies, waits for them, and re-layouts: 11.6 us -> 6.93 us
    ppermute x11 -> x9, starting transfers between devices: 17.7 us -> 13.5 us  [ring(): return lax.ppermute(value, 'frame', [(i, (i + by) % n) for i in range(n)])]
    ppermute x1, waiting for transfers between devices: 2.2 us -> 0.01 us  [across(): return lax.ppermute(value, ('frame', 'head'), pairs)]
    ppermute x1, waiting for transfers between devices: 0.01 us -> 2.07 us  [shards(): lax.ppermute(w_far, 'frame', [(i, (i // 16 ^ 1) * 16 + i % 16) for i in r...]
    ppermute x1, starting transfers between devices: 3.23 us -> 5.2 us  [shards(): lax.ppermute(w_far, 'frame', [(i, (i // 16 ^ 1) * 16 + i % 16) for i in r...]
    pallas_call x6 -> x7, Pallas kernels: 27.7 us -> 28.6 us  [kernel_call(): pl.pallas_call(body, in_specs=[SCALARS] * len(ints) + [ON_CHIP] * len(arg...]
  transfers between devices with their start and end apart: 20 -> 18, of which waited for: 9 -> 10; matrix products, arithmetic and copies ran while one was open for 6% -> 5% of each run, Pallas kernels for 13% -> 15%
where the time goes in v2:
time: 149 us
  waiting for transfers between devices  72.5 us (49%)
  starting transfers between devices  31.3 us (21%)
  Pallas kernels  28.6 us (19%)
  local copies, waits for them, and re-layouts  13.5 us (9%)
  between operations  2.12 us (1%)
    ppermute x9, waiting for transfers between devices, ring(): return lax.ppermute(value, 'frame', [(i, (i + by) % n) for i in range(n)])  44.7 us
    pallas_call x7, Pallas kernels, kernel_call(): pl.pallas_call(body, in_specs=[SCALARS] * len(ints) + [ON_CHIP] * len(arg...  28.6 us
    ppermute x7, waiting for transfers between devices, swap(): return lax.ppermute(value, 'head', pairs)  25.8 us
    ppermute x9, starting transfers between devices, ring(): return lax.ppermute(value, 'frame', [(i, (i + by) % n) for i in range(n)])  13.5 us
    ppermute x7, starting transfers between devices, swap(): return lax.ppermute(value, 'head', pairs)  9.68 us
    unnamed x30, local copies, waits for them, and re-layouts  6.93 us
    ppermute x1, starting transfers between devices, shards(): lax.ppermute(w_far, 'frame', [(i, (i // 16 ^ 1) * 16 + i % 16) for i in r...  5.2 us
    dynamic_slice x2, local copies, waits for them, and re-layouts, shards(): lax.dynamic_slice(weight, (0, at * width), (rows_w, width))  5 us
  transfers between devices with their start and end apart: 18, of which 10 were waited for; matrix products, arithmetic and copies ran while one was open for 5% of the time, Pallas kernels for 15%

profile of v2, /device:TPU:9, one launch (start us, length us, event | category | flops | bytes accessed | tf_op | source)
XLA Modules:
  0.0 148.8 jit_solution(15963263263572004063)
XLA Ops:
  0.6 6.5 %collective-permute-start.2 = (bf16[512,640]{1,0:T(8,128)(2,1)}, bf16[512,640]{1,0:T(8,128)(2,1)S(1)}, u32[]{:S(2)}, u32[]{:S(2)}) collective-permute-start(bf16[512,640]{1,0:T(8,128)(2,1)} %q_ref.1), channel_id=1, source_target_pairs={{0,252},{4,0},{8,4},{12,8},{16,12},{20,16},{24,20},{28,24},{32,28}... | collective-permute-start | bytes 1966088 | tf_op jit(solution)/shard_map/ppermute | solution.py:28
  7.1 2.9 %constant_dynamic-slice_fusion.2 = bf16[640,1280]{1,0:T(8,128)(2,1)} fusion(bf16[640,5120]{1,0:T(8,128)(2,1)} %param.13, s32[]{:T(128)S(6)} %select_n.31), kind=kLoop, calls=%fused_computation.4 | loop fusion | bytes 3276804 | tf_op jit(solution)/shard_map/dynamic_slice | solution.py:172
  10.0 2.9 %collective-permute-start.5 = (bf16[640,1280]{1,0:T(8,128)(2,1)}, bf16[640,1280]{1,0:T(8,128)(2,1)}, u32[]{:S(2)}, u32[]{:S(2)}) collective-permute-start(bf16[640,1280]{1,0:T(8,128)(2,1)} %constant_dynamic-slice_fusion.2), channel_id=1, source_target_pairs={{0,34},{1,35},{2,32},{3,33},{4,38},{5,39},{6,36},{7,37},{8,42},{9,... | collective-permute-start | bytes 4915208 | tf_op jit(solution)/shard_map/ppermute | solution.py:156
  13.8 2.0 %collective-permute-start.3 = (bf16[256,1280]{1,0:T(8,128)(2,1)S(1)}, bf16[256,1280]{1,0:T(8,128)(2,1)S(1)}, u32[]{:S(2)}, u32[]{:S(2)}) collective-permute-start(bf16[256,1280]{1,0:T(8,128)(2,1)S(1)} %get-tuple-element.47), channel_id=1, source_target_pairs={{0,252},{4,0},{8,4},{12,8},{16,12},{20,16},{24,20},{28,24},{32,28}... | collective-permute-start | bytes 1966088 | tf_op jit(solution)/shard_map/ppermute | solution.py:28
  16.5 4.1 %attend_own.1 = bf16[512,768]{1,0:T(8,128)(2,1)S(1)} custom-call(s32[5]{0:T(128)S(1)} %pad_add_fusion.meta, bf16[512,640]{1,0:T(8,128)(2,1)S(1)} %copy-done.7, bf16[512,640]{1,0:T(8,128)(2,1)S(1)} %copy-done.2, bf16[512,640]{1,0:T(8,128)(2,1)S(1)} %copy-done.3), custom_call_target="tpu_custom_call" | custom-call | flops 1 | bytes 1 | tf_op jit(solution)/shard_map/attend_own/pallas_call | solution.py:102
  21.6 4.1 %collective-permute-done.k2 = bf16[512,640]{1,0:T(8,128)(2,1)} collective-permute-done((bf16[512,640]{1,0:T(8,128)(2,1)}, bf16[512,640]{1,0:T(8,128)(2,1)}, u32[]{:S(2)}, u32[]{:S(2)}) %collective-permute-start) | collective-permute-done | bytes 655392 | tf_op jit(solution)/shard_map/ppermute | solution.py:28
  25.7 13.9 %collective-permute-done.1.v2 = bf16[512,640]{1,0:T(8,128)(2,1)S(1)} collective-permute-done((bf16[512,640]{1,0:T(8,128)(2,1)}, bf16[512,640]{1,0:T(8,128)(2,1)S(1)}, u32[]{:S(2)}, u32[]{:S(2)}) %collective-permute-start.1) | collective-permute-done | bytes 655392 | tf_op jit(solution)/shard_map/ppermute | solution.py:28
  42.0 15.8 %collective-permute-done.4.own = bf16[512,768]{1,0:T(8,128)(2,1)S(1)} collective-permute-done((bf16[512,768]{1,0:T(8,128)(2,1)S(1)}, bf16[512,768]{1,0:T(8,128)(2,1)S(1)}, u32[]{:S(2)}, u32[]{:S(2)}) %collective-permute-start.4) | collective-permute-done | bytes 786464 | tf_op jit(solution)/shard_map/ppermute | solution.py:28
  57.8 3.5 %collective-permute-start.8 = (bf16[256,1280]{1,0:T(8,128)(2,1)}, bf16[256,1280]{1,0:T(8,128)(2,1)S(1)}, u32[]{:S(2)}, u32[]{:S(2)}) collective-permute-start(bf16[256,1280]{1,0:T(8,128)(2,1)} %get-tuple-element.30), channel_id=1, source_target_pairs={{0,252},{4,0},{8,4},{12,8},{16,12},{20,16},{24,20},{28,24},{32,28}... | collective-permute-start | bytes 1966088 | tf_op jit(solution)/shard_map/ppermute | solution.py:28
  62.5 7.8 %attend_first.1 = (f32[512,640]{1,0:T(8,128)S(1)}, bf16[5,512,512]{2,1,0:T(8,128)(2,1)S(1)}) custom-call(s32[4]{0:T(128)S(1)} %fusion.allow, bf16[512,640]{1,0:T(8,128)(2,1)S(1)} %copy-done.6, bf16[512,768]{1,0:T(8,128)(2,1)S(1)} %collective-permute-done.4.own, bf16[512,640]{1,0:T(8,128)(2,1)S(1)} %copy-done.2, bf16[512,640]{1,0:T(8,128)(2,1)S(1)} %copy-done.3, ...), custom_call_target="tpu_custom_call" | custom-call | flops 1 | bytes 1 | tf_op jit(solution)/shard_map/attend_first/pallas_call | solution.py:102
  70.3 2.1 %constant_dynamic-slice_fusion = (bf16[640,1280]{1,0:T(8,128)(2,1)S(1)}, bf16[640,1280]{1,0:T(8,128)(2,1)S(1)}) fusion(bf16[640,5120]{1,0:T(8,128)(2,1)} %param.13, s32[]{:T(128)S(6)} %select_n.33, s32[]{:T(128)S(6)} %select_n.32), kind=kLoop, calls=%fused_computation.2 | loop fusion | bytes 6553608 | tf_op jit(solution)/shard_map/dynamic_slice | solution.py:172
  74.1 3.5 %collective-permute-start.12 = (bf16[640,1280]{1,0:T(8,128)(2,1)S(1)}, bf16[640,1280]{1,0:T(8,128)(2,1)S(1)}, u32[]{:S(2)}, u32[]{:S(2)}) collective-permute-start(bf16[640,1280]{1,0:T(8,128)(2,1)S(1)} %get-tuple-element.35), channel_id=1, source_target_pairs={{0,1},{1,0},{2,3},{3,2},{4,5},{5,4},{6,7},{7,6},{8,9},{9,8},{10,11... | collective-permute-start | bytes 4915208 | tf_op jit(solution)/shard_map/ppermute | solution.py:32
  77.6 2.4 %collective-permute-start.9 = (bf16[512,640]{1,0:T(8,128)(2,1)S(1)}, bf16[512,640]{1,0:T(8,128)(2,1)}, u32[]{:S(2)}, u32[]{:S(2)}) collective-permute-start(bf16[512,640]{1,0:T(8,128)(2,1)S(1)} %attend_last.1.a0), channel_id=1, source_target_pairs={{0,2},{2,0},{1,3},{3,1},{4,6},{6,4},{5,7},{7,5},{8,10},{10,8},{9,1... | collective-permute-start | bytes 1966088 | tf_op jit(solution)/shard_map/ppermute | solution.py:32
  80.1 5.2 %collective-permute-start.16 = (bf16[640,1280]{1,0:T(8,128)(2,1)}, bf16[640,1280]{1,0:T(8,128)(2,1)}, u32[]{:S(2)}, u32[]{:S(2)}) collective-permute-start(bf16[640,1280]{1,0:T(8,128)(2,1)} %collective-permute-done.5.w2), channel_id=1, source_target_pairs={{0,64},{4,68},{8,72},{12,76},{16,80},{20,84},{24,88},{28,92},{32,9... | collective-permute-start | bytes 4915208 | tf_op jit(solution)/shard_map/ppermute | solution.py:196
  85.3 2.2 %near_next.1.t = f32[512,1280]{1,0:T(8,128)S(1)} custom-call(bf16[512,640]{1,0:T(8,128)(2,1)S(1)} %attend_last.1.a0, bf16[512,640]{1,0:T(8,128)(2,1)S(1)} %collective-permute-done.11.a1, bf16[640,1280]{1,0:T(8,128)(2,1)S(1)} %get-tuple-element.34.w0, bf16[640,1280]{1,0:T(8,128)(2,1)S(1)} %collective-permute-done.12.w1), custom_call_target="tpu_custom_call" | custom-call | flops 1 | bytes 1 | tf_op jit(solution)/shard_map/near_next/pallas_call | solution.py:102
  87.5 10.1 %collective-permute-done.10.a0 = bf16[512,640]{1,0:T(8,128)(2,1)S(1)} collective-permute-done((bf16[512,640]{1,0:T(8,128)(2,1)S(1)}, bf16[512,640]{1,0:T(8,128)(2,1)S(1)}, u32[]{:S(2)}, u32[]{:S(2)}) %collective-permute-start.10) | collective-permute-done | bytes 655392 | tf_op jit(solution)/shard_map/ppermute | solution.py:28
  97.6 11.6 %collective-permute-done.9.a2 = bf16[512,640]{1,0:T(8,128)(2,1)} collective-permute-done((bf16[512,640]{1,0:T(8,128)(2,1)S(1)}, bf16[512,640]{1,0:T(8,128)(2,1)}, u32[]{:S(2)}, u32[]{:S(2)}) %collective-permute-start.9) | collective-permute-done | bytes 655392 | tf_op jit(solution)/shard_map/ppermute | solution.py:32
  112.2 2.2 %near_velocity.1.t = f32[512,1280]{1,0:T(8,128)S(1)} custom-call(bf16[512,640]{1,0:T(8,128)(2,1)S(1)} %collective-permute-done.10.a0, bf16[512,640]{1,0:T(8,128)(2,1)S(1)} %collective-permute-done.14.a1, bf16[640,1280]{1,0:T(8,128)(2,1)S(1)} %get-tuple-element.34.w0, bf16[640,1280]{1,0:T(8,128)(2,1)S(1)} %collective-permute-done.12.w1), custom_call_target="tpu_custom_call" | custom-call | flops 1 | bytes 1 | tf_op jit(solution)/shard_map/near_velocity/pallas_call | solution.py:102
  114.4 14.0 %collective-permute-done.13.a2 = bf16[512,640]{1,0:T(8,128)(2,1)} collective-permute-done((bf16[512,640]{1,0:T(8,128)(2,1)S(1)}, bf16[512,640]{1,0:T(8,128)(2,1)}, u32[]{:S(2)}, u32[]{:S(2)}) %collective-permute-start.13) | collective-permute-done | bytes 655392 | tf_op jit(solution)/shard_map/ppermute | solution.py:32
  131.2 2.1 %collective-permute-done.16.w3 = bf16[640,1280]{1,0:T(8,128)(2,1)} collective-permute-done((bf16[640,1280]{1,0:T(8,128)(2,1)}, bf16[640,1280]{1,0:T(8,128)(2,1)}, u32[]{:S(2)}, u32[]{:S(2)}) %collective-permute-start.16) | collective-permute-done | bytes 1638432 | tf_op jit(solution)/shard_map/ppermute | solution.py:196
  133.3 1.7 %copy-done.1 = f32[512,1280]{1,0:T(8,128)S(1)} copy-done((f32[512,1280]{1,0:T(8,128)S(1)}, f32[512,1280]{1,0:T(8,128)}, u32[]{:S(2)}) %copy-start.1) | copy-done | bytes 2621464
  135.0 1.3 copy-done.4
  137.4 5.8 %project_next.1 = bf16[512,1280]{1,0:T(8,128)(2,1)} custom-call(s32[3]{0:T(128)S(1)} %get-tuple-element.49.ints, f32[1]{0:T(128)S(6)} %sub.25.delta, f32[512,1280]{1,0:T(8,128)S(1)} %copy-done.1, bf16[512,640]{1,0:T(8,128)(2,1)} %collective-permute-done.9.a2, bf16[512,640]{1,0:T(8,128)(2,1)} %collective-permute-done.17.a3, ...), custom_call_target="tpu_custom_call" | custom-call | flops 1 | bytes 1 | tf_op jit(solution)/shard_map/project_next/pallas_call | solution.py:102
  143.2 5.6 %project_velocity.1 = bf16[512,1280]{1,0:T(8,128)(2,1)} custom-call(s32[3]{0:T(128)S(1)} %get-tuple-element.48.ints, f32[512,1280]{1,0:T(8,128)S(1)} %near_velocity.1.t, bf16[512,640]{1,0:T(8,128)(2,1)} %collective-permute-done.13.a2, bf16[512,640]{1,0:T(8,128)(2,1)} %collective-permute-done.15.a3, bf16[640,1280]{1,0:T(8,128)(2,1)} %collective-permute-done.5.w2, ...), custom_call_target="tpu_custom_call" | custom-call | flops 1 | bytes 1 | tf_op jit(solution)/shard_map/project_velocity/pallas_call | solution.py:102
  (57 shorter events, 13.3 us)
Async XLA Ops:
  0.6 20.2 %collective-permute-start.2 = (bf16[512,640]{1,0:T(8,128)(2,1)}, bf16[512,640]{1,0:T(8,128)(2,1)S(1)}, u32[]{:S(2)}, u32[]{:S(2)}) collective-permute-start(bf16[512,640]{1,0:T(8,128)(2,1)} %q_ref.1), channel_id=1, source_target_pairs={{0,252},{4,0},{8,4},{12,8},{16,12},{20,16},{24,20},{28,24},{32,28}... | collective-permute-start | bytes 1966088 | tf_op jit(solution)/shard_map/ppermute | solution.py:28
  7.1 18.6 %collective-permute-start = (bf16[512,640]{1,0:T(8,128)(2,1)}, bf16[512,640]{1,0:T(8,128)(2,1)}, u32[]{:S(2)}, u32[]{:S(2)}) collective-permute-start(bf16[512,640]{1,0:T(8,128)(2,1)} %k1.1), channel_id=1, source_target_pairs={{0,4},{4,8},{8,12},{12,16},{16,20},{20,24},{24,28},{28,32},{32,36}... | collective-permute-start | bytes 1966088 | tf_op jit(solution)/shard_map/ppermute | solution.py:28
  7.1 32.5 %collective-permute-start.1 = (bf16[512,640]{1,0:T(8,128)(2,1)}, bf16[512,640]{1,0:T(8,128)(2,1)S(1)}, u32[]{:S(2)}, u32[]{:S(2)}) collective-permute-start(bf16[512,640]{1,0:T(8,128)(2,1)} %v1.1), channel_id=1, source_target_pairs={{0,4},{4,8},{8,12},{12,16},{16,20},{20,24},{24,28},{28,32},{32,36}... | collective-permute-start | bytes 1966088 | tf_op jit(solution)/shard_map/ppermute | solution.py:28
  10.0 6.6 %copy-start.2 = (bf16[512,640]{1,0:T(8,128)(2,1)S(1)}, bf16[512,640]{1,0:T(8,128)(2,1)}, u32[]{:S(2)}) copy-start(bf16[512,640]{1,0:T(8,128)(2,1)} %k1.1) | copy-start | bytes 1966084
  10.0 6.6 %copy-start.3 = (bf16[512,640]{1,0:T(8,128)(2,1)S(1)}, bf16[512,640]{1,0:T(8,128)(2,1)}, u32[]{:S(2)}) copy-start(bf16[512,640]{1,0:T(8,128)(2,1)} %v1.1) | copy-start | bytes 1966084
  10.0 6.6 %copy-start.7 = (bf16[512,640]{1,0:T(8,128)(2,1)S(1)}, bf16[512,640]{1,0:T(8,128)(2,1)}, u32[]{:S(2)}) copy-start(bf16[512,640]{1,0:T(8,128)(2,1)} %q_ref.1) | copy-start | bytes 1966084
  10.0 47.8 %collective-permute-start.5 = (bf16[640,1280]{1,0:T(8,128)(2,1)}, bf16[640,1280]{1,0:T(8,128)(2,1)}, u32[]{:S(2)}, u32[]{:S(2)}) collective-permute-start(bf16[640,1280]{1,0:T(8,128)(2,1)} %constant_dynamic-slice_fusion.2), channel_id=1, source_target_pairs={{0,34},{1,35},{2,32},{3,33},{4,38},{5,39},{6,36},{7,37},{8,42},{9,... | collective-permute-start | bytes 4915208 | tf_op jit(solution)/shard_map/ppermute | solution.py:156
  13.8 25.9 %collective-permute-start.3 = (bf16[256,1280]{1,0:T(8,128)(2,1)S(1)}, bf16[256,1280]{1,0:T(8,128)(2,1)S(1)}, u32[]{:S(2)}, u32[]{:S(2)}) collective-permute-start(bf16[256,1280]{1,0:T(8,128)(2,1)S(1)} %get-tuple-element.47), channel_id=1, source_target_pairs={{0,252},{4,0},{8,4},{12,8},{16,12},{20,16},{24,20},{28,24},{32,28}... | collective-permute-start | bytes 1966088 | tf_op jit(solution)/shard_map/ppermute | solution.py:28
  40.5 17.3 %collective-permute-start.4 = (bf16[512,768]{1,0:T(8,128)(2,1)S(1)}, bf16[512,768]{1,0:T(8,128)(2,1)S(1)}, u32[]{:S(2)}, u32[]{:S(2)}) collective-permute-start(bf16[512,768]{1,0:T(8,128)(2,1)S(1)} %attend_own.1), channel_id=1, source_target_pairs={{0,252},{4,0},{8,4},{12,8},{16,12},{20,16},{24,20},{28,24},{32,28}... | collective-permute-start | bytes 2359304 | tf_op jit(solution)/shard_map/ppermute | solution.py:28
  40.8 20.6 %collective-permute-start.6 = (bf16[512,640]{1,0:T(8,128)(2,1)}, bf16[512,640]{1,0:T(8,128)(2,1)}, u32[]{:S(2)}, u32[]{:S(2)}) collective-permute-start(bf16[512,640]{1,0:T(8,128)(2,1)} %collective-permute-done.k2), channel_id=1, source_target_pairs={{0,4},{4,8},{8,12},{12,16},{16,20},{20,24},{24,28},{28,32},{32,36}... | collective-permute-start | bytes 1966088 | tf_op jit(solution)/shard_map/ppermute | solution.py:28
  42.0 30.5 %collective-permute-start.7 = (bf16[512,640]{1,0:T(8,128)(2,1)S(1)}, bf16[512,640]{1,0:T(8,128)(2,1)S(1)}, u32[]{:S(2)}, u32[]{:S(2)}) collective-permute-start(bf16[512,640]{1,0:T(8,128)(2,1)S(1)} %collective-permute-done.1.v2), channel_id=1, source_target_pairs={{0,4},{4,8},{8,12},{12,16},{16,20},{20,24},{24,28},{28,32},{32,36}... | collective-permute-start | bytes 1966088 | tf_op jit(solution)/shard_map/ppermute | solution.py:28
  57.8 15.4 %collective-permute-start.8 = (bf16[256,1280]{1,0:T(8,128)(2,1)}, bf16[256,1280]{1,0:T(8,128)(2,1)S(1)}, u32[]{:S(2)}, u32[]{:S(2)}) collective-permute-start(bf16[256,1280]{1,0:T(8,128)(2,1)} %get-tuple-element.30), channel_id=1, source_target_pairs={{0,252},{4,0},{8,4},{12,8},{16,12},{20,16},{24,20},{28,24},{32,28}... | collective-permute-start | bytes 1966088 | tf_op jit(solution)/shard_map/ppermute | solution.py:28
  74.1 11.2 %collective-permute-start.12 = (bf16[640,1280]{1,0:T(8,128)(2,1)S(1)}, bf16[640,1280]{1,0:T(8,128)(2,1)S(1)}, u32[]{:S(2)}, u32[]{:S(2)}) collective-permute-start(bf16[640,1280]{1,0:T(8,128)(2,1)S(1)} %get-tuple-element.35), channel_id=1, source_target_pairs={{0,1},{1,0},{2,3},{3,2},{4,5},{5,4},{6,7},{7,6},{8,9},{9,8},{10,11... | collective-permute-start | bytes 4915208 | tf_op jit(solution)/shard_map/ppermute | solution.py:32
  77.5 7.8 %collective-permute-start.11 = (bf16[512,640]{1,0:T(8,128)(2,1)S(1)}, bf16[512,640]{1,0:T(8,128)(2,1)S(1)}, u32[]{:S(2)}, u32[]{:S(2)}) collective-permute-start(bf16[512,640]{1,0:T(8,128)(2,1)S(1)} %attend_last.1.a0), channel_id=1, source_target_pairs={{0,1},{1,0},{2,3},{3,2},{4,5},{5,4},{6,7},{7,6},{8,9},{9,8},{10,11... | collective-permute-start | bytes 1966088 | tf_op jit(solution)/shard_map/ppermute | solution.py:32
  77.6 19.9 %collective-permute-start.10 = (bf16[512,640]{1,0:T(8,128)(2,1)S(1)}, bf16[512,640]{1,0:T(8,128)(2,1)S(1)}, u32[]{:S(2)}, u32[]{:S(2)}) collective-permute-start(bf16[512,640]{1,0:T(8,128)(2,1)S(1)} %attend_last.1.a0), channel_id=1, source_target_pairs={{0,4},{4,8},{8,12},{12,16},{16,20},{20,24},{24,28},{28,32},{32,36}... | collective-permute-start | bytes 1966088 | tf_op jit(solution)/shard_map/ppermute | solution.py:28
  77.6 31.6 %collective-permute-start.9 = (bf16[512,640]{1,0:T(8,128)(2,1)S(1)}, bf16[512,640]{1,0:T(8,128)(2,1)}, u32[]{:S(2)}, u32[]{:S(2)}) collective-permute-start(bf16[512,640]{1,0:T(8,128)(2,1)S(1)} %attend_last.1.a0), channel_id=1, source_target_pairs={{0,2},{2,0},{1,3},{3,1},{4,6},{6,4},{5,7},{7,5},{8,10},{10,8},{9,1... | collective-permute-start | bytes 1966088 | tf_op jit(solution)/shard_map/ppermute | solution.py:32
  80.1 53.2 %collective-permute-start.16 = (bf16[640,1280]{1,0:T(8,128)(2,1)}, bf16[640,1280]{1,0:T(8,128)(2,1)}, u32[]{:S(2)}, u32[]{:S(2)}) collective-permute-start(bf16[640,1280]{1,0:T(8,128)(2,1)} %collective-permute-done.5.w2), channel_id=1, source_target_pairs={{0,64},{4,68},{8,72},{12,76},{16,80},{20,84},{24,88},{28,92},{32,9... | collective-permute-start | bytes 4915208 | tf_op jit(solution)/shard_map/ppermute | solution.py:196
  87.5 26.9 %copy-start = (f32[512,1280]{1,0:T(8,128)}, f32[512,1280]{1,0:T(8,128)S(1)}, u32[]{:S(2)}) copy-start(f32[512,1280]{1,0:T(8,128)S(1)} %near_next.1.t) | copy-start | bytes 7864324
  87.5 45.8 %copy-start.9 = (bf16[256,1280]{1,0:T(8,128)(2,1)S(1)}, bf16[256,1280]{1,0:T(8,128)(2,1)}, u32[]{:S(2)}) copy-start(bf16[256,1280]{1,0:T(8,128)(2,1)} %copy-done.8) | copy-start | bytes 1966084
  87.5 45.8 %copy-start.12 = (f32[4,1280]{1,0:T(4,128)S(1)}, f32[4,1280]{1,0:T(4,128)}, u32[]{:S(2)}) copy-start(f32[4,1280]{1,0:T(4,128)} %gate.3) | copy-start | bytes 61444
  109.2 3.0 %collective-permute-start.14 = (bf16[512,640]{1,0:T(8,128)(2,1)S(1)}, bf16[512,640]{1,0:T(8,128)(2,1)S(1)}, u32[]{:S(2)}, u32[]{:S(2)}) collective-permute-start(bf16[512,640]{1,0:T(8,128)(2,1)S(1)} %collective-permute-done.10.a0), channel_id=1, source_target_pairs={{0,1},{1,0},{2,3},{3,2},{4,5},{5,4},{6,7},{7,6},{8,9},{9,8},{10,11... | collective-permute-start | bytes 1966088 | tf_op jit(solution)/shard_map/ppermute | solution.py:32
  110.4 18.0 %collective-permute-start.13 = (bf16[512,640]{1,0:T(8,128)(2,1)S(1)}, bf16[512,640]{1,0:T(8,128)(2,1)}, u32[]{:S(2)}, u32[]{:S(2)}) collective-permute-start(bf16[512,640]{1,0:T(8,128)(2,1)S(1)} %collective-permute-done.10.a0), channel_id=1, source_target_pairs={{0,2},{2,0},{1,3},{3,1},{4,6},{6,4},{5,7},{7,5},{8,10},{10,8},{9,1... | collective-permute-start | bytes 1966088 | tf_op jit(solution)/shard_map/ppermute | solution.py:32
  111.7 21.5 %collective-permute-start.17 = (bf16[512,640]{1,0:T(8,128)(2,1)}, bf16[512,640]{1,0:T(8,128)(2,1)}, u32[]{:S(2)}, u32[]{:S(2)}) collective-permute-start(bf16[512,640]{1,0:T(8,128)(2,1)} %collective-permute-done.9.a2), channel_id=1, source_target_pairs={{0,1},{1,0},{2,3},{3,2},{4,5},{5,4},{6,7},{7,6},{8,9},{9,8},{10,11... | collective-permute-start | bytes 1966088 | tf_op jit(solution)/shard_map/ppermute | solution.py:32
  128.4 14.8 %collective-permute-start.15 = (bf16[512,640]{1,0:T(8,128)(2,1)}, bf16[512,640]{1,0:T(8,128)(2,1)}, u32[]{:S(2)}, u32[]{:S(2)}) collective-permute-start(bf16[512,640]{1,0:T(8,128)(2,1)} %collective-permute-done.13.a2), channel_id=1, source_target_pairs={{0,1},{1,0},{2,3},{3,2},{4,5},{5,4},{6,7},{7,6},{8,9},{9,8},{10,11... | collective-permute-start | bytes 1966088 | tf_op jit(solution)/shard_map/ppermute | solution.py:32
  (9 other events, 20.0 us)

commit v3 on v2

--- a/solution.py
+++ b/solution.py
@@ -186,20 +186,20 @@
         4 * work * HD,
         work,
     )
-    k_r1, v_r1, q_next, lat_a, own = barrier((k_r1, v_r1, q_next, lat_a, own))
+    k_r1, v_r1, q_next, lat_a, own, w_own, w_sib = barrier(
+        (k_r1, v_r1, q_next, lat_a, own, columns_of(out_weight, head), columns_of(out_weight, head ^ 1))
+    )
 
     k_r2 = ring(k_r1, 1)
     v_r2 = ring(v_r1, 1)
     own = ring(own, -1)
-    own, w_far, lat_b, out_weight_ = barrier((own, w_far, latents[rows // 2 :], out_weight))
+    own, w_far, lat_b = barrier((own, w_far, latents[rows // 2 :]))
     lat_b = ring(lat_b, -1)
     w_far2 = lax.ppermute(
         w_far, "frame", [(i, (((i // 16) ^ 1) * 16) + i % 16) for i in range(NY * NXL * NZ)]
     )
     at = heads * HD + META
     meta_next = own[0, at : at + window + 1].astype(jnp.int32)
-    w_own = columns_of(out_weight_, head)
-    w_sib = columns_of(out_weight_, head ^ 1)
 
     span = lax.rem(frame + 1, spans)
     distances = jnp.arange(window, dtype=jnp.int32)
@@ -232,35 +232,37 @@
     near = jax.ShapeDtypeStruct((rows, width), F32)
     flops = 4 * rows * width * heads * HD
     (t1,) = kernel_call(project_near, (), (attended, sibling1, w_own, w_sib), (near,), "near_next", flops, space=24)
-    partner1, mine, t1 = barrier((partner1, mine, t1))
-    partner2 = swap(mine, PARTNER)
-    other1 = swap(partner1, SIBLING)
-    sibling2 = swap(mine, SIBLING)
-
     def scalars(level):
         at = level.astype(F32)
         delta = noise_level(at / LEVELS) - noise_level((at + 1.0) / LEVELS)
         is_last = (frame == spans - 1).astype(jnp.int32)
         return jnp.stack([level, odd, is_last]), delta[None]
 
+    ints1, delta = scalars(meta_next[window])
+    ints2, _ = scalars(levels[0])
+    partner1, mine, t1, ints1, delta, ints2 = barrier((partner1, mine, t1, ints1, delta, ints2))
+    partner2 = swap(mine, PARTNER)
+    sibling2 = swap(mine, SIBLING)
+    (t2,) = kernel_call(
+        project_near, (), (mine, sibling2, w_own, w_sib), (near,), "near_velocity", flops, space=24
+    )
+    other1 = swap(partner1, SIBLING)
     out = jax.ShapeDtypeStruct((rows, width), BF16)
-    ints, delta = scalars(meta_next[window])
     (next_latents,) = kernel_call(
         project_next,
-        (ints, delta),
+        (ints1, delta),
         (t1, partner1, other1, w_far, w_far2, gate_table, lat_a, lat_b, fresh),
         (out,),
         "project_next",
         flops,
         space=24,
     )
-    (t2,) = kernel_call(project_near, (), (mine, sibling2, w_own, w_sib), (near,), "near_velocity", flops, space=24)
     partner2, t2 = barrier((partner2, t2))
-    ints, _ = scalars(levels[0])
+    other2 = swap(partner2, SIBLING)
     (velocity,) = kernel_call(
         project_velocity,
-        (ints,),
-        (t2, partner2, swap(partner2, SIBLING), w_far, w_far2, gate_table),
+        (ints2,),
+        (t2, partner2, other2, w_far, w_far2, gate_table),
         (out,),
         "project_velocity",
         flops,

time: 149 us -> 148 us (level)
  local copies, waits for them, and re-layouts: 13.5 us -> 6.44 us
  Pallas kernels: 28.6 us -> 33.2 us
  starting transfers between devices: 31.3 us -> 35 us
  waiting for transfers between devices: 72.5 us -> 69.4 us
    ppermute x9, waiting for transfers between devices: 44.7 us -> 33.7 us  [ring(): return lax.ppermute(value, 'frame', [(i, (i + by) % n) for i in range(n)])]
    unnamed x30 -> x18, local copies, waits for them, and re-layouts: 6.93 us -> 0.86 us
    ppermute x7, waiting for transfers between devices: 25.8 us -> 30.7 us  [swap(): return lax.ppermute(value, 'head', pairs)]
    pallas_call x7, Pallas kernels: 28.6 us -> 33.2 us  [kernel_call(): pl.pallas_call(body, in_specs=[SCALARS] * len(ints) + [ON_CHIP] * len(arg...]
    ppermute x1, waiting for transfers between devices: 2.07 us -> 4.93 us  [shards(): lax.ppermute(w_far, 'frame', [(i, (i // 16 ^ 1) * 16 + i % 16) for i in r...]
    ppermute x9, starting transfers between devices: 13.5 us -> 16.1 us  [ring(): return lax.ppermute(value, 'frame', [(i, (i + by) % n) for i in range(n)])]
    dynamic_slice x2 -> x1, local copies, waits for them, and re-layouts: 5 us -> 4.02 us  [shards(): lax.dynamic_slice(weight, (0, at * width), (rows_w, width))]
  transfers between devices with their start and end apart: 18 -> 18, of which waited for: 10 -> 8; matrix products, arithmetic and copies ran while one was open for 5% -> 5% of each run, Pallas kernels for 15% -> 17%
where the time goes in v3:
time: 148 us
  waiting for transfers between devices  69.4 us (47%)
  starting transfers between devices  35 us (24%)
  Pallas kernels  33.2 us (22%)
  local copies, waits for them, and re-layouts  6.44 us (4%)
  between operations  2.13 us (1%)
  other arithmetic  1.57 us (1%)
    ppermute x9, waiting for transfers between devices, ring(): return lax.ppermute(value, 'frame', [(i, (i + by) % n) for i in range(n)])  33.7 us
    pallas_call x7, Pallas kernels, kernel_call(): pl.pallas_call(body, in_specs=[SCALARS] * len(ints) + [ON_CHIP] * len(arg...  33.2 us
    ppermute x7, waiting for transfers between devices, swap(): return lax.ppermute(value, 'head', pairs)  30.7 us
    ppermute x9, starting transfers between devices, ring(): return lax.ppermute(value, 'frame', [(i, (i + by) % n) for i in range(n)])  16.1 us
    ppermute x7, starting transfers between devices, swap(): return lax.ppermute(value, 'head', pairs)  10 us
    ppermute x1, starting transfers between devices, shards(): lax.ppermute(w_far, 'frame', [(i, (i // 16 ^ 1) * 16 + i % 16) for i in r...  6.03 us
    ppermute x1, waiting for transfers between devices, shards(): lax.ppermute(w_far, 'frame', [(i, (i // 16 ^ 1) * 16 + i % 16) for i in r...  4.93 us
    dynamic_slice x1, local copies, waits for them, and re-layouts, shards(): lax.dynamic_slice(weight, (0, at * width), (rows_w, width))  4.02 us
  transfers between devices with their start and end apart: 18, of which 8 were waited for; matrix products, arithmetic and copies ran while one was open for 5% of the time, Pallas kernels for 17%

profile of v3, /device:TPU:9, one launch (start us, length us, event | category | flops | bytes accessed | tf_op | source)
XLA Modules:
  0.0 147.7 jit_solution(15350544907738618485)
XLA Ops:
  0.6 1.7 %collective-permute-start = (bf16[512,640]{1,0:T(8,128)(2,1)}, bf16[512,640]{1,0:T(8,128)(2,1)}, u32[]{:S(2)}, u32[]{:S(2)}) collective-permute-start(bf16[512,640]{1,0:T(8,128)(2,1)} %k1.1), channel_id=1, source_target_pairs={{0,4},{4,8},{8,12},{12,16},{16,20},{20,24},{24,28},{28,32},{32,36}... | collective-permute-start | bytes 1966088 | tf_op jit(solution)/shard_map/ppermute | solution.py:28
  4.0 3.3 %collective-permute-start.2 = (bf16[512,640]{1,0:T(8,128)(2,1)}, bf16[512,640]{1,0:T(8,128)(2,1)}, u32[]{:S(2)}, u32[]{:S(2)}) collective-permute-start(bf16[512,640]{1,0:T(8,128)(2,1)} %q_ref.1), channel_id=1, source_target_pairs={{0,252},{4,0},{8,4},{12,8},{16,12},{20,16},{24,20},{28,24},{32,28}... | collective-permute-start | bytes 1966088 | tf_op jit(solution)/shard_map/ppermute | solution.py:28
  7.3 4.0 %constant_dynamic-slice_fusion = (bf16[640,1280]{1,0:T(8,128)(2,1)S(1)}, bf16[640,1280]{1,0:T(8,128)(2,1)S(1)}, bf16[640,1280]{1,0:T(8,128)(2,1)}) fusion(bf16[640,5120]{1,0:T(8,128)(2,1)} %param.13, s32[]{:T(128)S(6)} %select_n.33, s32[]{:T(128)S(6)} %select_n.27, s32[]{:T(128)S(6)} %select_n.28), kind=kLoop, calls=%fused_computation.2 | loop fusion | bytes 9830412 | tf_op jit(solution)/shard_map/dynamic_slice | solution.py:172
  11.3 2.9 %collective-permute-start.5 = (bf16[640,1280]{1,0:T(8,128)(2,1)S(1)}, bf16[640,1280]{1,0:T(8,128)(2,1)}, u32[]{:S(2)}, u32[]{:S(2)}) collective-permute-start(bf16[640,1280]{1,0:T(8,128)(2,1)S(1)} %get-tuple-element.52), channel_id=1, source_target_pairs={{0,34},{1,35},{2,32},{3,33},{4,38},{5,39},{6,36},{7,37},{8,42},{9,... | collective-permute-start | bytes 4915208 | tf_op jit(solution)/shard_map/ppermute | solution.py:156
  15.9 4.1 %attend_own.1 = bf16[512,768]{1,0:T(8,128)(2,1)S(1)} custom-call(s32[5]{0:T(128)S(1)} %pad_add_fusion.meta, bf16[512,640]{1,0:T(8,128)(2,1)S(1)} %copy-done.3, bf16[512,640]{1,0:T(8,128)(2,1)S(1)} %copy-done, bf16[512,640]{1,0:T(8,128)(2,1)S(1)} %copy-done.1), custom_call_target="tpu_custom_call" | custom-call | flops 1 | bytes 1 | tf_op jit(solution)/shard_map/attend_own/pallas_call | solution.py:102
  20.0 1.9 %collective-permute-done.k2 = bf16[512,640]{1,0:T(8,128)(2,1)} collective-permute-done((bf16[512,640]{1,0:T(8,128)(2,1)}, bf16[512,640]{1,0:T(8,128)(2,1)}, u32[]{:S(2)}, u32[]{:S(2)}) %collective-permute-start) | collective-permute-done | bytes 655392 | tf_op jit(solution)/shard_map/ppermute | solution.py:28
  21.9 14.0 %collective-permute-done.1.v2 = bf16[512,640]{1,0:T(8,128)(2,1)} collective-permute-done((bf16[512,640]{1,0:T(8,128)(2,1)}, bf16[512,640]{1,0:T(8,128)(2,1)}, u32[]{:S(2)}, u32[]{:S(2)}) %collective-permute-start.1) | collective-permute-done | bytes 655392 | tf_op jit(solution)/shard_map/ppermute | solution.py:28
  36.8 4.1 %collective-permute-start.4 = (bf16[512,768]{1,0:T(8,128)(2,1)S(1)}, bf16[512,768]{1,0:T(8,128)(2,1)}, u32[]{:S(2)}, u32[]{:S(2)}) collective-permute-start(bf16[512,768]{1,0:T(8,128)(2,1)S(1)} %attend_own.1), channel_id=1, source_target_pairs={{0,252},{4,0},{8,4},{12,8},{16,12},{20,16},{24,20},{28,24},{32,28}... | collective-permute-start | bytes 2359304 | tf_op jit(solution)/shard_map/ppermute | solution.py:28
  40.9 15.2 %collective-permute-done.4.own = bf16[512,768]{1,0:T(8,128)(2,1)} collective-permute-done((bf16[512,768]{1,0:T(8,128)(2,1)S(1)}, bf16[512,768]{1,0:T(8,128)(2,1)}, u32[]{:S(2)}, u32[]{:S(2)}) %collective-permute-start.4) | collective-permute-done | bytes 786464 | tf_op jit(solution)/shard_map/ppermute | solution.py:28
  56.1 5.3 %collective-permute-start.8 = (bf16[256,1280]{1,0:T(8,128)(2,1)}, bf16[256,1280]{1,0:T(8,128)(2,1)}, u32[]{:S(2)}, u32[]{:S(2)}) collective-permute-start(bf16[256,1280]{1,0:T(8,128)(2,1)} %get-tuple-element.34), channel_id=1, source_target_pairs={{0,252},{4,0},{8,4},{12,8},{16,12},{20,16},{24,20},{28,24},{32,28}... | collective-permute-start | bytes 1966088 | tf_op jit(solution)/shard_map/ppermute | solution.py:28
  62.1 8.4 %attend_first.1 = (f32[512,640]{1,0:T(8,128)S(1)}, bf16[5,512,512]{2,1,0:T(8,128)(2,1)S(1)}) custom-call(s32[4]{0:T(128)S(1)} %fusion.allow, bf16[512,640]{1,0:T(8,128)(2,1)} %collective-permute-done.2.q_ref, bf16[512,768]{1,0:T(8,128)(2,1)} %collective-permute-done.4.own, bf16[512,640]{1,0:T(8,128)(2,1)S(1)} %copy-done, bf16[512,640]{1,0:T(8,128)(2,1)S(1)} %copy-done.1, ...), custom_call_target="tpu_custom_call" | custom-call | flops 1 | bytes 1 | tf_op jit(solution)/shard_map/attend_first/pallas_call | solution.py:102
  70.5 2.0 %collective-permute-done.7.v3 = bf16[512,640]{1,0:T(8,128)(2,1)} collective-permute-done((bf16[512,640]{1,0:T(8,128)(2,1)}, bf16[512,640]{1,0:T(8,128)(2,1)}, u32[]{:S(2)}, u32[]{:S(2)}) %collective-permute-start.7) | collective-permute-done | bytes 655392 | tf_op jit(solution)/shard_map/ppermute | solution.py:28
  73.1 2.8 %attend_last.1.a0 = bf16[512,640]{1,0:T(8,128)(2,1)} custom-call(f32[512,640]{1,0:T(8,128)S(1)} %get-tuple-element.32.acc_ref, bf16[5,512,512]{2,1,0:T(8,128)(2,1)S(1)} %get-tuple-element.33.p_ref, bf16[512,640]{1,0:T(8,128)(2,1)} %collective-permute-done.7.v3), custom_call_target="tpu_custom_call" | custom-call | flops 1 | bytes 1 | tf_op jit(solution)/shard_map/attend_last/pallas_call | solution.py:102
  75.9 3.5 %collective-permute-start.12 = (bf16[640,1280]{1,0:T(8,128)(2,1)}, bf16[640,1280]{1,0:T(8,128)(2,1)S(1)}, u32[]{:S(2)}, u32[]{:S(2)}) collective-permute-start(bf16[640,1280]{1,0:T(8,128)(2,1)} %get-tuple-element.40), channel_id=1, source_target_pairs={{0,1},{1,0},{2,3},{3,2},{4,5},{5,4},{6,7},{7,6},{8,9},{9,8},{10,11... | collective-permute-start | bytes 4915208 | tf_op jit(solution)/shard_map/ppermute | solution.py:32
  79.4 1.8 %collective-permute-start.9 = (bf16[512,640]{1,0:T(8,128)(2,1)}, bf16[512,640]{1,0:T(8,128)(2,1)}, u32[]{:S(2)}, u32[]{:S(2)}) collective-permute-start(bf16[512,640]{1,0:T(8,128)(2,1)} %attend_last.1.a0), channel_id=1, source_target_pairs={{0,2},{2,0},{1,3},{3,1},{4,6},{6,4},{5,7},{7,5},{8,10},{10,8},{9,1... | collective-permute-start | bytes 1966088 | tf_op jit(solution)/shard_map/ppermute | solution.py:32
  81.2 6.0 %collective-permute-start.16 = (bf16[640,1280]{1,0:T(8,128)(2,1)}, bf16[640,1280]{1,0:T(8,128)(2,1)}, u32[]{:S(2)}, u32[]{:S(2)}) collective-permute-start(bf16[640,1280]{1,0:T(8,128)(2,1)} %collective-permute-done.5.w2), channel_id=1, source_target_pairs={{0,64},{4,68},{8,72},{12,76},{16,80},{20,84},{24,88},{28,92},{32,9... | collective-permute-start | bytes 4915208 | tf_op jit(solution)/shard_map/ppermute | solution.py:198
  89.4 3.5 %near_next.1.t = f32[512,1280]{1,0:T(8,128)S(1)} custom-call(bf16[512,640]{1,0:T(8,128)(2,1)} %attend_last.1.a0, bf16[512,640]{1,0:T(8,128)(2,1)} %collective-permute-done.11.a1, bf16[640,1280]{1,0:T(8,128)(2,1)S(1)} %get-tuple-element.39.w0, bf16[640,1280]{1,0:T(8,128)(2,1)S(1)} %collective-permute-done.12.w1), custom_call_target="tpu_custom_call" | custom-call | flops 1 | bytes 1 | tf_op jit(solution)/shard_map/near_next/pallas_call | solution.py:102
  92.9 18.2 %collective-permute-done.9.a2 = bf16[512,640]{1,0:T(8,128)(2,1)} collective-permute-done((bf16[512,640]{1,0:T(8,128)(2,1)}, bf16[512,640]{1,0:T(8,128)(2,1)}, u32[]{:S(2)}, u32[]{:S(2)}) %collective-permute-start.9) | collective-permute-done | bytes 655392 | tf_op jit(solution)/shard_map/ppermute | solution.py:32
  112.7 1.8 %collective-permute-start.13 = (bf16[512,640]{1,0:T(8,128)(2,1)}, bf16[512,640]{1,0:T(8,128)(2,1)S(1)}, u32[]{:S(2)}, u32[]{:S(2)}) collective-permute-start(bf16[512,640]{1,0:T(8,128)(2,1)} %collective-permute-done.10.a0), channel_id=1, source_target_pairs={{0,2},{2,0},{1,3},{3,1},{4,6},{6,4},{5,7},{7,5},{8,10},{10,8},{9,1... | collective-permute-start | bytes 1966088 | tf_op jit(solution)/shard_map/ppermute | solution.py:32
  114.9 3.3 %near_velocity.1.t = f32[512,1280]{1,0:T(8,128)S(1)} custom-call(bf16[512,640]{1,0:T(8,128)(2,1)} %collective-permute-done.10.a0, bf16[512,640]{1,0:T(8,128)(2,1)S(1)} %collective-permute-done.14.a1, bf16[640,1280]{1,0:T(8,128)(2,1)S(1)} %get-tuple-element.39.w0, bf16[640,1280]{1,0:T(8,128)(2,1)S(1)} %collective-permute-done.12.w1), custom_call_target="tpu_custom_call" | custom-call | flops 1 | bytes 1 | tf_op jit(solution)/shard_map/near_velocity/pallas_call | solution.py:102
  118.2 12.5 %collective-permute-done.13.a2 = bf16[512,640]{1,0:T(8,128)(2,1)S(1)} collective-permute-done((bf16[512,640]{1,0:T(8,128)(2,1)}, bf16[512,640]{1,0:T(8,128)(2,1)S(1)}, u32[]{:S(2)}, u32[]{:S(2)}) %collective-permute-start.13) | collective-permute-done | bytes 655392 | tf_op jit(solution)/shard_map/ppermute | solution.py:32
  131.6 4.9 %collective-permute-done.16.w3 = bf16[640,1280]{1,0:T(8,128)(2,1)} collective-permute-done((bf16[640,1280]{1,0:T(8,128)(2,1)}, bf16[640,1280]{1,0:T(8,128)(2,1)}, u32[]{:S(2)}, u32[]{:S(2)}) %collective-permute-start.16) | collective-permute-done | bytes 1638432 | tf_op jit(solution)/shard_map/ppermute | solution.py:198
  136.6 5.9 %project_next.1 = bf16[512,1280]{1,0:T(8,128)(2,1)} custom-call(s32[3]{0:T(128)S(1)} %get-tuple-element.46.ints, f32[1]{0:T(128)S(6)} %sub.25.delta, f32[512,1280]{1,0:T(8,128)S(1)} %near_next.1.t, bf16[512,640]{1,0:T(8,128)(2,1)} %collective-permute-done.9.a2, bf16[512,640]{1,0:T(8,128)(2,1)S(1)} %collective-permute-done.17.a3, ...), custom_call_target="tpu_custom_call" | custom-call | flops 1 | bytes 1 | tf_op jit(solution)/shard_map/project_next/pallas_call | solution.py:102
  142.4 5.3 %project_velocity.1 = bf16[512,1280]{1,0:T(8,128)(2,1)} custom-call(s32[3]{0:T(128)S(1)} %get-tuple-element.41.ints, f32[512,1280]{1,0:T(8,128)S(1)} %near_velocity.1.t, bf16[512,640]{1,0:T(8,128)(2,1)S(1)} %collective-permute-done.13.a2, bf16[512,640]{1,0:T(8,128)(2,1)S(1)} %collective-permute-done.15.a3, bf16[640,1280]{1,0:T(8,128)(2,1)} %collective-permute-done.5.w2, ...), custom_call_target="tpu_custom_call" | custom-call | flops 1 | bytes 1 | tf_op jit(solution)/shard_map/project_velocity/pallas_call | solution.py:102
  (44 shorter events, 9.2 us)
Async XLA Ops:
  0.6 21.2 %collective-permute-start = (bf16[512,640]{1,0:T(8,128)(2,1)}, bf16[512,640]{1,0:T(8,128)(2,1)}, u32[]{:S(2)}, u32[]{:S(2)}) collective-permute-start(bf16[512,640]{1,0:T(8,128)(2,1)} %k1.1), channel_id=1, source_target_pairs={{0,4},{4,8},{8,12},{12,16},{16,20},{20,24},{24,28},{28,32},{32,36}... | collective-permute-start | bytes 1966088 | tf_op jit(solution)/shard_map/ppermute | solution.py:28
  2.3 33.6 %collective-permute-start.1 = (bf16[512,640]{1,0:T(8,128)(2,1)}, bf16[512,640]{1,0:T(8,128)(2,1)}, u32[]{:S(2)}, u32[]{:S(2)}) collective-permute-start(bf16[512,640]{1,0:T(8,128)(2,1)} %v1.1), channel_id=1, source_target_pairs={{0,4},{4,8},{8,12},{12,16},{16,20},{20,24},{24,28},{28,32},{32,36}... | collective-permute-start | bytes 1966088 | tf_op jit(solution)/shard_map/ppermute | solution.py:28
  4.0 31.9 %collective-permute-start.2 = (bf16[512,640]{1,0:T(8,128)(2,1)}, bf16[512,640]{1,0:T(8,128)(2,1)}, u32[]{:S(2)}, u32[]{:S(2)}) collective-permute-start(bf16[512,640]{1,0:T(8,128)(2,1)} %q_ref.1), channel_id=1, source_target_pairs={{0,252},{4,0},{8,4},{12,8},{16,12},{20,16},{24,20},{28,24},{32,28}... | collective-permute-start | bytes 1966088 | tf_op jit(solution)/shard_map/ppermute | solution.py:28
  7.3 6.9 %copy-start.7 = (bf16[512,1280]{1,0:T(8,128)(2,1)S(1)}, bf16[512,1280]{1,0:T(8,128)(2,1)}, u32[]{:S(2)}) copy-start(bf16[512,1280]{1,0:T(8,128)(2,1)} %param.9) | copy-start | bytes 3932164
  11.3 4.5 %copy-start.1 = (bf16[512,640]{1,0:T(8,128)(2,1)S(1)}, bf16[512,640]{1,0:T(8,128)(2,1)}, u32[]{:S(2)}) copy-start(bf16[512,640]{1,0:T(8,128)(2,1)} %v1.1) | copy-start | bytes 1966084
  11.3 4.5 %copy-start.3 = (bf16[512,640]{1,0:T(8,128)(2,1)S(1)}, bf16[512,640]{1,0:T(8,128)(2,1)}, u32[]{:S(2)}) copy-start(bf16[512,640]{1,0:T(8,128)(2,1)} %q_ref.1) | copy-start | bytes 1966084
  11.3 44.7 %collective-permute-start.5 = (bf16[640,1280]{1,0:T(8,128)(2,1)S(1)}, bf16[640,1280]{1,0:T(8,128)(2,1)}, u32[]{:S(2)}, u32[]{:S(2)}) collective-permute-start(bf16[640,1280]{1,0:T(8,128)(2,1)S(1)} %get-tuple-element.52), channel_id=1, source_target_pairs={{0,34},{1,35},{2,32},{3,33},{4,38},{5,39},{6,36},{7,37},{8,42},{9,... | collective-permute-start | bytes 4915208 | tf_op jit(solution)/shard_map/ppermute | solution.py:156
  15.1 20.8 %collective-permute-start.3 = (bf16[256,1280]{1,0:T(8,128)(2,1)S(1)}, bf16[256,1280]{1,0:T(8,128)(2,1)S(1)}, u32[]{:S(2)}, u32[]{:S(2)}) collective-permute-start(bf16[256,1280]{1,0:T(8,128)(2,1)S(1)} %get-tuple-element.56), channel_id=1, source_target_pairs={{0,252},{4,0},{8,4},{12,8},{16,12},{20,16},{24,20},{28,24},{32,28}... | collective-permute-start | bytes 1966088 | tf_op jit(solution)/shard_map/ppermute | solution.py:28
  36.8 19.3 %collective-permute-start.4 = (bf16[512,768]{1,0:T(8,128)(2,1)S(1)}, bf16[512,768]{1,0:T(8,128)(2,1)}, u32[]{:S(2)}, u32[]{:S(2)}) collective-permute-start(bf16[512,768]{1,0:T(8,128)(2,1)S(1)} %attend_own.1), channel_id=1, source_target_pairs={{0,252},{4,0},{8,4},{12,8},{16,12},{20,16},{24,20},{28,24},{32,28}... | collective-permute-start | bytes 2359304 | tf_op jit(solution)/shard_map/ppermute | solution.py:28
  40.9 21.3 %collective-permute-start.6 = (bf16[512,640]{1,0:T(8,128)(2,1)}, bf16[512,640]{1,0:T(8,128)(2,1)}, u32[]{:S(2)}, u32[]{:S(2)}) collective-permute-start(bf16[512,640]{1,0:T(8,128)(2,1)} %collective-permute-done.k2), channel_id=1, source_target_pairs={{0,4},{4,8},{8,12},{12,16},{16,20},{20,24},{24,28},{28,32},{32,36}... | collective-permute-start | bytes 1966088 | tf_op jit(solution)/shard_map/ppermute | solution.py:28
  40.9 31.7 %collective-permute-start.7 = (bf16[512,640]{1,0:T(8,128)(2,1)}, bf16[512,640]{1,0:T(8,128)(2,1)}, u32[]{:S(2)}, u32[]{:S(2)}) collective-permute-start(bf16[512,640]{1,0:T(8,128)(2,1)} %collective-permute-done.1.v2), channel_id=1, source_target_pairs={{0,4},{4,8},{8,12},{12,16},{16,20},{20,24},{24,28},{28,32},{32,36}... | collective-permute-start | bytes 1966088 | tf_op jit(solution)/shard_map/ppermute | solution.py:28
  56.1 17.1 %collective-permute-start.8 = (bf16[256,1280]{1,0:T(8,128)(2,1)}, bf16[256,1280]{1,0:T(8,128)(2,1)}, u32[]{:S(2)}, u32[]{:S(2)}) collective-permute-start(bf16[256,1280]{1,0:T(8,128)(2,1)} %get-tuple-element.34), channel_id=1, source_target_pairs={{0,252},{4,0},{8,4},{12,8},{16,12},{20,16},{24,20},{28,24},{32,28}... | collective-permute-start | bytes 1966088 | tf_op jit(solution)/shard_map/ppermute | solution.py:28
  75.9 13.5 %collective-permute-start.12 = (bf16[640,1280]{1,0:T(8,128)(2,1)}, bf16[640,1280]{1,0:T(8,128)(2,1)S(1)}, u32[]{:S(2)}, u32[]{:S(2)}) collective-permute-start(bf16[640,1280]{1,0:T(8,128)(2,1)} %get-tuple-element.40), channel_id=1, source_target_pairs={{0,1},{1,0},{2,3},{3,2},{4,5},{5,4},{6,7},{7,6},{8,9},{9,8},{10,11... | collective-permute-start | bytes 4915208 | tf_op jit(solution)/shard_map/ppermute | solution.py:32
  79.4 10.0 %collective-permute-start.11 = (bf16[512,640]{1,0:T(8,128)(2,1)}, bf16[512,640]{1,0:T(8,128)(2,1)}, u32[]{:S(2)}, u32[]{:S(2)}) collective-permute-start(bf16[512,640]{1,0:T(8,128)(2,1)} %attend_last.1.a0), channel_id=1, source_target_pairs={{0,1},{1,0},{2,3},{3,2},{4,5},{5,4},{6,7},{7,6},{8,9},{9,8},{10,11... | collective-permute-start | bytes 1966088 | tf_op jit(solution)/shard_map/ppermute | solution.py:32
  79.4 31.7 %collective-permute-start.9 = (bf16[512,640]{1,0:T(8,128)(2,1)}, bf16[512,640]{1,0:T(8,128)(2,1)}, u32[]{:S(2)}, u32[]{:S(2)}) collective-permute-start(bf16[512,640]{1,0:T(8,128)(2,1)} %attend_last.1.a0), channel_id=1, source_target_pairs={{0,2},{2,0},{1,3},{3,1},{4,6},{6,4},{5,7},{7,5},{8,10},{10,8},{9,1... | collective-permute-start | bytes 1966088 | tf_op jit(solution)/shard_map/ppermute | solution.py:32
  81.2 29.9 %collective-permute-start.10 = (bf16[512,640]{1,0:T(8,128)(2,1)}, bf16[512,640]{1,0:T(8,128)(2,1)}, u32[]{:S(2)}, u32[]{:S(2)}) collective-permute-start(bf16[512,640]{1,0:T(8,128)(2,1)} %attend_last.1.a0), channel_id=1, source_target_pairs={{0,4},{4,8},{8,12},{12,16},{16,20},{20,24},{24,28},{28,32},{32,36}... | collective-permute-start | bytes 1966088 | tf_op jit(solution)/shard_map/ppermute | solution.py:28
  81.2 55.4 %collective-permute-start.16 = (bf16[640,1280]{1,0:T(8,128)(2,1)}, bf16[640,1280]{1,0:T(8,128)(2,1)}, u32[]{:S(2)}, u32[]{:S(2)}) collective-permute-start(bf16[640,1280]{1,0:T(8,128)(2,1)} %collective-permute-done.5.w2), channel_id=1, source_target_pairs={{0,64},{4,68},{8,72},{12,76},{16,80},{20,84},{24,88},{28,92},{32,9... | collective-permute-start | bytes 4915208 | tf_op jit(solution)/shard_map/ppermute | solution.py:198
  111.1 25.5 %copy-start.2 = (bf16[512,1280]{1,0:T(8,128)(2,1)S(1)}, bf16[512,1280]{1,0:T(8,128)(2,1)}, u32[]{:S(2)}) copy-start(bf16[512,1280]{1,0:T(8,128)(2,1)} %fresh.1) | copy-start | bytes 3932164
  111.1 25.5 %copy-start.5 = (bf16[256,1280]{1,0:T(8,128)(2,1)S(1)}, bf16[256,1280]{1,0:T(8,128)(2,1)}, u32[]{:S(2)}) copy-start(bf16[256,1280]{1,0:T(8,128)(2,1)} %copy-done.4) | copy-start | bytes 1966084
  111.1 25.5 %copy-start.6 = (f32[4,1280]{1,0:T(4,128)S(1)}, f32[4,1280]{1,0:T(4,128)}, u32[]{:S(2)}) copy-start(f32[4,1280]{1,0:T(4,128)} %gate.3) | copy-start | bytes 61444
  111.1 3.8 %collective-permute-start.14 = (bf16[512,640]{1,0:T(8,128)(2,1)}, bf16[512,640]{1,0:T(8,128)(2,1)S(1)}, u32[]{:S(2)}, u32[]{:S(2)}) collective-permute-start(bf16[512,640]{1,0:T(8,128)(2,1)} %collective-permute-done.10.a0), channel_id=1, source_target_pairs={{0,1},{1,0},{2,3},{3,2},{4,5},{5,4},{6,7},{7,6},{8,9},{9,8},{10,11... | collective-permute-start | bytes 1966088 | tf_op jit(solution)/shard_map/ppermute | solution.py:32
  112.7 18.0 %collective-permute-start.13 = (bf16[512,640]{1,0:T(8,128)(2,1)}, bf16[512,640]{1,0:T(8,128)(2,1)S(1)}, u32[]{:S(2)}, u32[]{:S(2)}) collective-permute-start(bf16[512,640]{1,0:T(8,128)(2,1)} %collective-permute-done.10.a0), channel_id=1, source_target_pairs={{0,2},{2,0},{1,3},{3,1},{4,6},{6,4},{5,7},{7,5},{8,10},{10,8},{9,1... | collective-permute-start | bytes 1966088 | tf_op jit(solution)/shard_map/ppermute | solution.py:32
  114.6 22.0 %collective-permute-start.17 = (bf16[512,640]{1,0:T(8,128)(2,1)}, bf16[512,640]{1,0:T(8,128)(2,1)S(1)}, u32[]{:S(2)}, u32[]{:S(2)}) collective-permute-start(bf16[512,640]{1,0:T(8,128)(2,1)} %collective-permute-done.9.a2), channel_id=1, source_target_pairs={{0,1},{1,0},{2,3},{3,2},{4,5},{5,4},{6,7},{7,6},{8,9},{9,8},{10,11... | collective-permute-start | bytes 1966088 | tf_op jit(solution)/shard_map/ppermute | solution.py:32
  130.8 11.7 %collective-permute-start.15 = (bf16[512,640]{1,0:T(8,128)(2,1)S(1)}, bf16[512,640]{1,0:T(8,128)(2,1)S(1)}, u32[]{:S(2)}, u32[]{:S(2)}) collective-permute-start(bf16[512,640]{1,0:T(8,128)(2,1)S(1)} %collective-permute-done.13.a2), channel_id=1, source_target_pairs={{0,1},{1,0},{2,3},{3,2},{4,5},{5,4},{6,7},{7,6},{8,9},{9,8},{10,11... | collective-permute-start | bytes 1966088 | tf_op jit(solution)/shard_map/ppermute | solution.py:32
  (3 other events, 9.8 us)

commit v4 on v3

--- a/solution.py
+++ b/solution.py
@@ -115,27 +115,30 @@
     t[...] += jnp.dot(a1[...], w1[...], preferred_element_type=F32)
 
 
-def project_far(ints, t, a2, a3, w2, w3, gate, columns):
-    k = a2.shape[1]
+def in_order(ints, a2, a3):
     swapped = ints[1] == 1
-    x2 = jnp.where(swapped, a3[...], a2[...])
-    x3 = jnp.where(swapped, a2[...], a3[...])
+    return jnp.where(swapped, a3[...], a2[...]), jnp.where(swapped, a2[...], a3[...])
+
+
+def project_far(ints, t, x2, x3, w2, w3, gate, columns):
     total = t[:, columns] + jnp.dot(x2, w2[:, columns], preferred_element_type=F32)
     total += jnp.dot(x3, w3[:, columns], preferred_element_type=F32)
     return gate[pl.ds(ints[0], 1), columns] * total
 
 
 def project_velocity(ints, t, a2, a3, w2, w3, gate, out):
+    x2, x3 = in_order(ints, a2, a3)
     for j in range(out.shape[1] // CHUNK):
         columns = pl.ds(j * CHUNK, CHUNK)
-        out[:, columns] = project_far(ints, t, a2, a3, w2, w3, gate, columns).astype(BF16)
+        out[:, columns] = project_far(ints, t, x2, x3, w2, w3, gate, columns).astype(BF16)
 
 
 def project_next(ints, delta, t, a2, a3, w2, w3, gate, lat_a, lat_b, fresh, out):
+    x2, x3 = in_order(ints, a2, a3)
     half = lat_a.shape[0]
     for j in range(out.shape[1] // CHUNK):
         columns = pl.ds(j * CHUNK, CHUNK)
-        update = delta[0] * project_far(ints, t, a2, a3, w2, w3, gate, columns)
+        update = delta[0] * project_far(ints, t, x2, x3, w2, w3, gate, columns)
         for i, lat in enumerate((lat_a, lat_b)):
             rows = pl.ds(i * half, half)
             new = (lat[:, columns].astype(F32) + update[i * half : (i + 1) * half]).astype(BF16)

time: 148 us -> 148 us (level)
  no operation moved by 1% of the time
where the time goes in v4:
time: 148 us; the launch traced here: 147 us
  waiting for transfers between devices  69.4 us (47%)
  starting transfers between devices  35 us (24%)
  Pallas kernels  33 us (22%)
  local copies, waits for them, and re-layouts  6.44 us (4%)
  between operations  2.13 us (1%)
  other arithmetic  1.57 us (1%)
    ppermute x9, waiting for transfers between devices, ring(): return lax.ppermute(value, 'frame', [(i, (i + by) % n) for i in range(n)])  33.7 us
    pallas_call x7, Pallas kernels, kernel_call(): pl.pallas_call(body, in_specs=[SCALARS] * len(ints) + [ON_CHIP] * len(arg...  33 us
    ppermute x7, waiting for transfers between devices, swap(): return lax.ppermute(value, 'head', pairs)  30.7 us
    ppermute x9, starting transfers between devices, ring(): return lax.ppermute(value, 'frame', [(i, (i + by) % n) for i in range(n)])  16.1 us
    ppermute x7, starting transfers between devices, swap(): return lax.ppermute(value, 'head', pairs)  10 us
    ppermute x1, starting transfers between devices, shards(): lax.ppermute(w_far, 'frame', [(i, (i // 16 ^ 1) * 16 + i % 16) for i in r...  6.03 us
    ppermute x1, waiting for transfers between devices, shards(): lax.ppermute(w_far, 'frame', [(i, (i // 16 ^ 1) * 16 + i % 16) for i in r...  4.93 us
    dynamic_slice x1, local copies, waits for them, and re-layouts, shards(): lax.dynamic_slice(weight, (0, at * width), (rows_w, width))  4.02 us
  transfers between devices with their start and end apart: 18, of which 8 were waited for; matrix products, arithmetic and copies ran while one was open for 5% of the time, Pallas kernels for 17%

profile of v4, /device:TPU:9, one launch (start us, length us, event | category | flops | bytes accessed | tf_op | source)
XLA Modules:
  0.0 147.5 jit_solution(450449913051957874)
XLA Ops:
  0.6 1.7 %collective-permute-start = (bf16[512,640]{1,0:T(8,128)(2,1)}, bf16[512,640]{1,0:T(8,128)(2,1)}, u32[]{:S(2)}, u32[]{:S(2)}) collective-permute-start(bf16[512,640]{1,0:T(8,128)(2,1)} %k1.1), channel_id=1, source_target_pairs={{0,4},{4,8},{8,12},{12,16},{16,20},{20,24},{24,28},{28,32},{32,36}... | collective-permute-start | bytes 1966088 | tf_op jit(solution)/shard_map/ppermute | solution.py:28
  4.0 3.3 %collective-permute-start.2 = (bf16[512,640]{1,0:T(8,128)(2,1)}, bf16[512,640]{1,0:T(8,128)(2,1)}, u32[]{:S(2)}, u32[]{:S(2)}) collective-permute-start(bf16[512,640]{1,0:T(8,128)(2,1)} %q_ref.1), channel_id=1, source_target_pairs={{0,252},{4,0},{8,4},{12,8},{16,12},{20,16},{24,20},{28,24},{32,28}... | collective-permute-start | bytes 1966088 | tf_op jit(solution)/shard_map/ppermute | solution.py:28
  7.3 4.0 %constant_dynamic-slice_fusion = (bf16[640,1280]{1,0:T(8,128)(2,1)S(1)}, bf16[640,1280]{1,0:T(8,128)(2,1)S(1)}, bf16[640,1280]{1,0:T(8,128)(2,1)}) fusion(bf16[640,5120]{1,0:T(8,128)(2,1)} %param.13, s32[]{:T(128)S(6)} %select_n.33, s32[]{:T(128)S(6)} %select_n.27, s32[]{:T(128)S(6)} %select_n.28), kind=kLoop, calls=%fused_computation.2 | loop fusion | bytes 9830412 | tf_op jit(solution)/shard_map/dynamic_slice | solution.py:175
  11.3 2.9 %collective-permute-start.5 = (bf16[640,1280]{1,0:T(8,128)(2,1)S(1)}, bf16[640,1280]{1,0:T(8,128)(2,1)}, u32[]{:S(2)}, u32[]{:S(2)}) collective-permute-start(bf16[640,1280]{1,0:T(8,128)(2,1)S(1)} %get-tuple-element.52), channel_id=1, source_target_pairs={{0,34},{1,35},{2,32},{3,33},{4,38},{5,39},{6,36},{7,37},{8,42},{9,... | collective-permute-start | bytes 4915208 | tf_op jit(solution)/shard_map/ppermute | solution.py:159
  15.9 4.1 %attend_own.1 = bf16[512,768]{1,0:T(8,128)(2,1)S(1)} custom-call(s32[5]{0:T(128)S(1)} %pad_add_fusion.meta, bf16[512,640]{1,0:T(8,128)(2,1)S(1)} %copy-done.3, bf16[512,640]{1,0:T(8,128)(2,1)S(1)} %copy-done, bf16[512,640]{1,0:T(8,128)(2,1)S(1)} %copy-done.1), custom_call_target="tpu_custom_call" | custom-call | flops 1 | bytes 1 | tf_op jit(solution)/shard_map/attend_own/pallas_call | solution.py:102
  20.0 1.9 %collective-permute-done.k2 = bf16[512,640]{1,0:T(8,128)(2,1)} collective-permute-done((bf16[512,640]{1,0:T(8,128)(2,1)}, bf16[512,640]{1,0:T(8,128)(2,1)}, u32[]{:S(2)}, u32[]{:S(2)}) %collective-permute-start) | collective-permute-done | bytes 655392 | tf_op jit(solution)/shard_map/ppermute | solution.py:28
  21.9 14.0 %collective-permute-done.1.v2 = bf16[512,640]{1,0:T(8,128)(2,1)} collective-permute-done((bf16[512,640]{1,0:T(8,128)(2,1)}, bf16[512,640]{1,0:T(8,128)(2,1)}, u32[]{:S(2)}, u32[]{:S(2)}) %collective-permute-start.1) | collective-permute-done | bytes 655392 | tf_op jit(solution)/shard_map/ppermute | solution.py:28
  36.8 4.1 %collective-permute-start.4 = (bf16[512,768]{1,0:T(8,128)(2,1)S(1)}, bf16[512,768]{1,0:T(8,128)(2,1)}, u32[]{:S(2)}, u32[]{:S(2)}) collective-permute-start(bf16[512,768]{1,0:T(8,128)(2,1)S(1)} %attend_own.1), channel_id=1, source_target_pairs={{0,252},{4,0},{8,4},{12,8},{16,12},{20,16},{24,20},{28,24},{32,28}... | collective-permute-start | bytes 2359304 | tf_op jit(solution)/shard_map/ppermute | solution.py:28
  40.9 15.2 %collective-permute-done.4.own = bf16[512,768]{1,0:T(8,128)(2,1)} collective-permute-done((bf16[512,768]{1,0:T(8,128)(2,1)S(1)}, bf16[512,768]{1,0:T(8,128)(2,1)}, u32[]{:S(2)}, u32[]{:S(2)}) %collective-permute-start.4) | collective-permute-done | bytes 786464 | tf_op jit(solution)/shard_map/ppermute | solution.py:28
  56.1 5.3 %collective-permute-start.8 = (bf16[256,1280]{1,0:T(8,128)(2,1)}, bf16[256,1280]{1,0:T(8,128)(2,1)}, u32[]{:S(2)}, u32[]{:S(2)}) collective-permute-start(bf16[256,1280]{1,0:T(8,128)(2,1)} %get-tuple-element.34), channel_id=1, source_target_pairs={{0,252},{4,0},{8,4},{12,8},{16,12},{20,16},{24,20},{28,24},{32,28}... | collective-permute-start | bytes 1966088 | tf_op jit(solution)/shard_map/ppermute | solution.py:28
  62.1 8.4 %attend_first.1 = (f32[512,640]{1,0:T(8,128)S(1)}, bf16[5,512,512]{2,1,0:T(8,128)(2,1)S(1)}) custom-call(s32[4]{0:T(128)S(1)} %fusion.allow, bf16[512,640]{1,0:T(8,128)(2,1)} %collective-permute-done.2.q_ref, bf16[512,768]{1,0:T(8,128)(2,1)} %collective-permute-done.4.own, bf16[512,640]{1,0:T(8,128)(2,1)S(1)} %copy-done, bf16[512,640]{1,0:T(8,128)(2,1)S(1)} %copy-done.1, ...), custom_call_target="tpu_custom_call" | custom-call | flops 1 | bytes 1 | tf_op jit(solution)/shard_map/attend_first/pallas_call | solution.py:102
  70.5 2.0 %collective-permute-done.7.v3 = bf16[512,640]{1,0:T(8,128)(2,1)} collective-permute-done((bf16[512,640]{1,0:T(8,128)(2,1)}, bf16[512,640]{1,0:T(8,128)(2,1)}, u32[]{:S(2)}, u32[]{:S(2)}) %collective-permute-start.7) | collective-permute-done | bytes 655392 | tf_op jit(solution)/shard_map/ppermute | solution.py:28
  73.1 2.8 %attend_last.1.a0 = bf16[512,640]{1,0:T(8,128)(2,1)} custom-call(f32[512,640]{1,0:T(8,128)S(1)} %get-tuple-element.32.acc_ref, bf16[5,512,512]{2,1,0:T(8,128)(2,1)S(1)} %get-tuple-element.33.p_ref, bf16[512,640]{1,0:T(8,128)(2,1)} %collective-permute-done.7.v3), custom_call_target="tpu_custom_call" | custom-call | flops 1 | bytes 1 | tf_op jit(solution)/shard_map/attend_last/pallas_call | solution.py:102
  75.9 3.5 %collective-permute-start.12 = (bf16[640,1280]{1,0:T(8,128)(2,1)}, bf16[640,1280]{1,0:T(8,128)(2,1)S(1)}, u32[]{:S(2)}, u32[]{:S(2)}) collective-permute-start(bf16[640,1280]{1,0:T(8,128)(2,1)} %get-tuple-element.40), channel_id=1, source_target_pairs={{0,1},{1,0},{2,3},{3,2},{4,5},{5,4},{6,7},{7,6},{8,9},{9,8},{10,11... | collective-permute-start | bytes 4915208 | tf_op jit(solution)/shard_map/ppermute | solution.py:32
  79.4 1.8 %collective-permute-start.9 = (bf16[512,640]{1,0:T(8,128)(2,1)}, bf16[512,640]{1,0:T(8,128)(2,1)}, u32[]{:S(2)}, u32[]{:S(2)}) collective-permute-start(bf16[512,640]{1,0:T(8,128)(2,1)} %attend_last.1.a0), channel_id=1, source_target_pairs={{0,2},{2,0},{1,3},{3,1},{4,6},{6,4},{5,7},{7,5},{8,10},{10,8},{9,1... | collective-permute-start | bytes 1966088 | tf_op jit(solution)/shard_map/ppermute | solution.py:32
  81.2 6.0 %collective-permute-start.16 = (bf16[640,1280]{1,0:T(8,128)(2,1)}, bf16[640,1280]{1,0:T(8,128)(2,1)}, u32[]{:S(2)}, u32[]{:S(2)}) collective-permute-start(bf16[640,1280]{1,0:T(8,128)(2,1)} %collective-permute-done.5.w2), channel_id=1, source_target_pairs={{0,64},{4,68},{8,72},{12,76},{16,80},{20,84},{24,88},{28,92},{32,9... | collective-permute-start | bytes 4915208 | tf_op jit(solution)/shard_map/ppermute | solution.py:201
  89.4 3.5 %near_next.1.t = f32[512,1280]{1,0:T(8,128)S(1)} custom-call(bf16[512,640]{1,0:T(8,128)(2,1)} %attend_last.1.a0, bf16[512,640]{1,0:T(8,128)(2,1)} %collective-permute-done.11.a1, bf16[640,1280]{1,0:T(8,128)(2,1)S(1)} %get-tuple-element.39.w0, bf16[640,1280]{1,0:T(8,128)(2,1)S(1)} %collective-permute-done.12.w1), custom_call_target="tpu_custom_call" | custom-call | flops 1 | bytes 1 | tf_op jit(solution)/shard_map/near_next/pallas_call | solution.py:102
  92.9 18.2 %collective-permute-done.9.a2 = bf16[512,640]{1,0:T(8,128)(2,1)} collective-permute-done((bf16[512,640]{1,0:T(8,128)(2,1)}, bf16[512,640]{1,0:T(8,128)(2,1)}, u32[]{:S(2)}, u32[]{:S(2)}) %collective-permute-start.9) | collective-permute-done | bytes 655392 | tf_op jit(solution)/shard_map/ppermute | solution.py:32
  112.7 1.8 %collective-permute-start.13 = (bf16[512,640]{1,0:T(8,128)(2,1)}, bf16[512,640]{1,0:T(8,128)(2,1)S(1)}, u32[]{:S(2)}, u32[]{:S(2)}) collective-permute-start(bf16[512,640]{1,0:T(8,128)(2,1)} %collective-permute-done.10.a0), channel_id=1, source_target_pairs={{0,2},{2,0},{1,3},{3,1},{4,6},{6,4},{5,7},{7,5},{8,10},{10,8},{9,1... | collective-permute-start | bytes 1966088 | tf_op jit(solution)/shard_map/ppermute | solution.py:32
  114.9 3.3 %near_velocity.1.t = f32[512,1280]{1,0:T(8,128)S(1)} custom-call(bf16[512,640]{1,0:T(8,128)(2,1)} %collective-permute-done.10.a0, bf16[512,640]{1,0:T(8,128)(2,1)S(1)} %collective-permute-done.14.a1, bf16[640,1280]{1,0:T(8,128)(2,1)S(1)} %get-tuple-element.39.w0, bf16[640,1280]{1,0:T(8,128)(2,1)S(1)} %collective-permute-done.12.w1), custom_call_target="tpu_custom_call" | custom-call | flops 1 | bytes 1 | tf_op jit(solution)/shard_map/near_velocity/pallas_call | solution.py:102
  118.2 12.5 %collective-permute-done.13.a2 = bf16[512,640]{1,0:T(8,128)(2,1)S(1)} collective-permute-done((bf16[512,640]{1,0:T(8,128)(2,1)}, bf16[512,640]{1,0:T(8,128)(2,1)S(1)}, u32[]{:S(2)}, u32[]{:S(2)}) %collective-permute-start.13) | collective-permute-done | bytes 655392 | tf_op jit(solution)/shard_map/ppermute | solution.py:32
  131.6 4.9 %collective-permute-done.16.w3 = bf16[640,1280]{1,0:T(8,128)(2,1)} collective-permute-done((bf16[640,1280]{1,0:T(8,128)(2,1)}, bf16[640,1280]{1,0:T(8,128)(2,1)}, u32[]{:S(2)}, u32[]{:S(2)}) %collective-permute-start.16) | collective-permute-done | bytes 1638432 | tf_op jit(solution)/shard_map/ppermute | solution.py:201
  136.6 5.7 %project_next.1 = bf16[512,1280]{1,0:T(8,128)(2,1)} custom-call(s32[3]{0:T(128)S(1)} %get-tuple-element.46.ints, f32[1]{0:T(128)S(6)} %sub.25.delta, f32[512,1280]{1,0:T(8,128)S(1)} %near_next.1.t, bf16[512,640]{1,0:T(8,128)(2,1)} %collective-permute-done.9.a2, bf16[512,640]{1,0:T(8,128)(2,1)S(1)} %collective-permute-done.17.a3, ...), custom_call_target="tpu_custom_call" | custom-call | flops 1 | bytes 1 | tf_op jit(solution)/shard_map/project_next/pallas_call | solution.py:102
  142.3 5.2 %project_velocity.1 = bf16[512,1280]{1,0:T(8,128)(2,1)} custom-call(s32[3]{0:T(128)S(1)} %get-tuple-element.41.ints, f32[512,1280]{1,0:T(8,128)S(1)} %near_velocity.1.t, bf16[512,640]{1,0:T(8,128)(2,1)S(1)} %collective-permute-done.13.a2, bf16[512,640]{1,0:T(8,128)(2,1)S(1)} %collective-permute-done.15.a3, bf16[640,1280]{1,0:T(8,128)(2,1)} %collective-permute-done.5.w2, ...), custom_call_target="tpu_custom_call" | custom-call | flops 1 | bytes 1 | tf_op jit(solution)/shard_map/project_velocity/pallas_call | solution.py:102
  (44 shorter events, 9.2 us)
Async XLA Ops:
  0.6 21.2 %collective-permute-start = (bf16[512,640]{1,0:T(8,128)(2,1)}, bf16[512,640]{1,0:T(8,128)(2,1)}, u32[]{:S(2)}, u32[]{:S(2)}) collective-permute-start(bf16[512,640]{1,0:T(8,128)(2,1)} %k1.1), channel_id=1, source_target_pairs={{0,4},{4,8},{8,12},{12,16},{16,20},{20,24},{24,28},{28,32},{32,36}... | collective-permute-start | bytes 1966088 | tf_op jit(solution)/shard_map/ppermute | solution.py:28
  2.3 33.6 %collective-permute-start.1 = (bf16[512,640]{1,0:T(8,128)(2,1)}, bf16[512,640]{1,0:T(8,128)(2,1)}, u32[]{:S(2)}, u32[]{:S(2)}) collective-permute-start(bf16[512,640]{1,0:T(8,128)(2,1)} %v1.1), channel_id=1, source_target_pairs={{0,4},{4,8},{8,12},{12,16},{16,20},{20,24},{24,28},{28,32},{32,36}... | collective-permute-start | bytes 1966088 | tf_op jit(solution)/shard_map/ppermute | solution.py:28
  4.0 31.9 %collective-permute-start.2 = (bf16[512,640]{1,0:T(8,128)(2,1)}, bf16[512,640]{1,0:T(8,128)(2,1)}, u32[]{:S(2)}, u32[]{:S(2)}) collective-permute-start(bf16[512,640]{1,0:T(8,128)(2,1)} %q_ref.1), channel_id=1, source_target_pairs={{0,252},{4,0},{8,4},{12,8},{16,12},{20,16},{24,20},{28,24},{32,28}... | collective-permute-start | bytes 1966088 | tf_op jit(solution)/shard_map/ppermute | solution.py:28
  7.3 6.9 %copy-start.7 = (bf16[512,1280]{1,0:T(8,128)(2,1)S(1)}, bf16[512,1280]{1,0:T(8,128)(2,1)}, u32[]{:S(2)}) copy-start(bf16[512,1280]{1,0:T(8,128)(2,1)} %param.9) | copy-start | bytes 3932164
  11.3 4.5 %copy-start.1 = (bf16[512,640]{1,0:T(8,128)(2,1)S(1)}, bf16[512,640]{1,0:T(8,128)(2,1)}, u32[]{:S(2)}) copy-start(bf16[512,640]{1,0:T(8,128)(2,1)} %v1.1) | copy-start | bytes 1966084
  11.3 4.5 %copy-start.3 = (bf16[512,640]{1,0:T(8,128)(2,1)S(1)}, bf16[512,640]{1,0:T(8,128)(2,1)}, u32[]{:S(2)}) copy-start(bf16[512,640]{1,0:T(8,128)(2,1)} %q_ref.1) | copy-start | bytes 1966084
  11.3 44.7 %collective-permute-start.5 = (bf16[640,1280]{1,0:T(8,128)(2,1)S(1)}, bf16[640,1280]{1,0:T(8,128)(2,1)}, u32[]{:S(2)}, u32[]{:S(2)}) collective-permute-start(bf16[640,1280]{1,0:T(8,128)(2,1)S(1)} %get-tuple-element.52), channel_id=1, source_target_pairs={{0,34},{1,35},{2,32},{3,33},{4,38},{5,39},{6,36},{7,37},{8,42},{9,... | collective-permute-start | bytes 4915208 | tf_op jit(solution)/shard_map/ppermute | solution.py:159
  15.1 20.8 %collective-permute-start.3 = (bf16[256,1280]{1,0:T(8,128)(2,1)S(1)}, bf16[256,1280]{1,0:T(8,128)(2,1)S(1)}, u32[]{:S(2)}, u32[]{:S(2)}) collective-permute-start(bf16[256,1280]{1,0:T(8,128)(2,1)S(1)} %get-tuple-element.56), channel_id=1, source_target_pairs={{0,252},{4,0},{8,4},{12,8},{16,12},{20,16},{24,20},{28,24},{32,28}... | collective-permute-start | bytes 1966088 | tf_op jit(solution)/shard_map/ppermute | solution.py:28
  36.8 19.3 %collective-permute-start.4 = (bf16[512,768]{1,0:T(8,128)(2,1)S(1)}, bf16[512,768]{1,0:T(8,128)(2,1)}, u32[]{:S(2)}, u32[]{:S(2)}) collective-permute-start(bf16[512,768]{1,0:T(8,128)(2,1)S(1)} %attend_own.1), channel_id=1, source_target_pairs={{0,252},{4,0},{8,4},{12,8},{16,12},{20,16},{24,20},{28,24},{32,28}... | collective-permute-start | bytes 2359304 | tf_op jit(solution)/shard_map/ppermute | solution.py:28
  40.9 21.3 %collective-permute-start.6 = (bf16[512,640]{1,0:T(8,128)(2,1)}, bf16[512,640]{1,0:T(8,128)(2,1)}, u32[]{:S(2)}, u32[]{:S(2)}) collective-permute-start(bf16[512,640]{1,0:T(8,128)(2,1)} %collective-permute-done.k2), channel_id=1, source_target_pairs={{0,4},{4,8},{8,12},{12,16},{16,20},{20,24},{24,28},{28,32},{32,36}... | collective-permute-start | bytes 1966088 | tf_op jit(solution)/shard_map/ppermute | solution.py:28
  40.9 31.7 %collective-permute-start.7 = (bf16[512,640]{1,0:T(8,128)(2,1)}, bf16[512,640]{1,0:T(8,128)(2,1)}, u32[]{:S(2)}, u32[]{:S(2)}) collective-permute-start(bf16[512,640]{1,0:T(8,128)(2,1)} %collective-permute-done.1.v2), channel_id=1, source_target_pairs={{0,4},{4,8},{8,12},{12,16},{16,20},{20,24},{24,28},{28,32},{32,36}... | collective-permute-start | bytes 1966088 | tf_op jit(solution)/shard_map/ppermute | solution.py:28
  56.1 17.1 %collective-permute-start.8 = (bf16[256,1280]{1,0:T(8,128)(2,1)}, bf16[256,1280]{1,0:T(8,128)(2,1)}, u32[]{:S(2)}, u32[]{:S(2)}) collective-permute-start(bf16[256,1280]{1,0:T(8,128)(2,1)} %get-tuple-element.34), channel_id=1, source_target_pairs={{0,252},{4,0},{8,4},{12,8},{16,12},{20,16},{24,20},{28,24},{32,28}... | collective-permute-start | bytes 1966088 | tf_op jit(solution)/shard_map/ppermute | solution.py:28
  75.9 13.5 %collective-permute-start.12 = (bf16[640,1280]{1,0:T(8,128)(2,1)}, bf16[640,1280]{1,0:T(8,128)(2,1)S(1)}, u32[]{:S(2)}, u32[]{:S(2)}) collective-permute-start(bf16[640,1280]{1,0:T(8,128)(2,1)} %get-tuple-element.40), channel_id=1, source_target_pairs={{0,1},{1,0},{2,3},{3,2},{4,5},{5,4},{6,7},{7,6},{8,9},{9,8},{10,11... | collective-permute-start | bytes 4915208 | tf_op jit(solution)/shard_map/ppermute | solution.py:32
  79.4 10.0 %collective-permute-start.11 = (bf16[512,640]{1,0:T(8,128)(2,1)}, bf16[512,640]{1,0:T(8,128)(2,1)}, u32[]{:S(2)}, u32[]{:S(2)}) collective-permute-start(bf16[512,640]{1,0:T(8,128)(2,1)} %attend_last.1.a0), channel_id=1, source_target_pairs={{0,1},{1,0},{2,3},{3,2},{4,5},{5,4},{6,7},{7,6},{8,9},{9,8},{10,11... | collective-permute-start | bytes 1966088 | tf_op jit(solution)/shard_map/ppermute | solution.py:32
  79.4 31.7 %collective-permute-start.9 = (bf16[512,640]{1,0:T(8,128)(2,1)}, bf16[512,640]{1,0:T(8,128)(2,1)}, u32[]{:S(2)}, u32[]{:S(2)}) collective-permute-start(bf16[512,640]{1,0:T(8,128)(2,1)} %attend_last.1.a0), channel_id=1, source_target_pairs={{0,2},{2,0},{1,3},{3,1},{4,6},{6,4},{5,7},{7,5},{8,10},{10,8},{9,1... | collective-permute-start | bytes 1966088 | tf_op jit(solution)/shard_map/ppermute | solution.py:32
  81.2 29.9 %collective-permute-start.10 = (bf16[512,640]{1,0:T(8,128)(2,1)}, bf16[512,640]{1,0:T(8,128)(2,1)}, u32[]{:S(2)}, u32[]{:S(2)}) collective-permute-start(bf16[512,640]{1,0:T(8,128)(2,1)} %attend_last.1.a0), channel_id=1, source_target_pairs={{0,4},{4,8},{8,12},{12,16},{16,20},{20,24},{24,28},{28,32},{32,36}... | collective-permute-start | bytes 1966088 | tf_op jit(solution)/shard_map/ppermute | solution.py:28
  81.2 55.4 %collective-permute-start.16 = (bf16[640,1280]{1,0:T(8,128)(2,1)}, bf16[640,1280]{1,0:T(8,128)(2,1)}, u32[]{:S(2)}, u32[]{:S(2)}) collective-permute-start(bf16[640,1280]{1,0:T(8,128)(2,1)} %collective-permute-done.5.w2), channel_id=1, source_target_pairs={{0,64},{4,68},{8,72},{12,76},{16,80},{20,84},{24,88},{28,92},{32,9... | collective-permute-start | bytes 4915208 | tf_op jit(solution)/shard_map/ppermute | solution.py:201
  111.1 25.5 %copy-start.2 = (bf16[512,1280]{1,0:T(8,128)(2,1)S(1)}, bf16[512,1280]{1,0:T(8,128)(2,1)}, u32[]{:S(2)}) copy-start(bf16[512,1280]{1,0:T(8,128)(2,1)} %fresh.1) | copy-start | bytes 3932164
  111.1 25.5 %copy-start.5 = (bf16[256,1280]{1,0:T(8,128)(2,1)S(1)}, bf16[256,1280]{1,0:T(8,128)(2,1)}, u32[]{:S(2)}) copy-start(bf16[256,1280]{1,0:T(8,128)(2,1)} %copy-done.4) | copy-start | bytes 1966084
  111.1 25.5 %copy-start.6 = (f32[4,1280]{1,0:T(4,128)S(1)}, f32[4,1280]{1,0:T(4,128)}, u32[]{:S(2)}) copy-start(f32[4,1280]{1,0:T(4,128)} %gate.3) | copy-start | bytes 61444
  111.1 3.8 %collective-permute-start.14 = (bf16[512,640]{1,0:T(8,128)(2,1)}, bf16[512,640]{1,0:T(8,128)(2,1)S(1)}, u32[]{:S(2)}, u32[]{:S(2)}) collective-permute-start(bf16[512,640]{1,0:T(8,128)(2,1)} %collective-permute-done.10.a0), channel_id=1, source_target_pairs={{0,1},{1,0},{2,3},{3,2},{4,5},{5,4},{6,7},{7,6},{8,9},{9,8},{10,11... | collective-permute-start | bytes 1966088 | tf_op jit(solution)/shard_map/ppermute | solution.py:32
  112.7 18.0 %collective-permute-start.13 = (bf16[512,640]{1,0:T(8,128)(2,1)}, bf16[512,640]{1,0:T(8,128)(2,1)S(1)}, u32[]{:S(2)}, u32[]{:S(2)}) collective-permute-start(bf16[512,640]{1,0:T(8,128)(2,1)} %collective-permute-done.10.a0), channel_id=1, source_target_pairs={{0,2},{2,0},{1,3},{3,1},{4,6},{6,4},{5,7},{7,5},{8,10},{10,8},{9,1... | collective-permute-start | bytes 1966088 | tf_op jit(solution)/shard_map/ppermute | solution.py:32
  114.6 22.0 %collective-permute-start.17 = (bf16[512,640]{1,0:T(8,128)(2,1)}, bf16[512,640]{1,0:T(8,128)(2,1)S(1)}, u32[]{:S(2)}, u32[]{:S(2)}) collective-permute-start(bf16[512,640]{1,0:T(8,128)(2,1)} %collective-permute-done.9.a2), channel_id=1, source_target_pairs={{0,1},{1,0},{2,3},{3,2},{4,5},{5,4},{6,7},{7,6},{8,9},{9,8},{10,11... | collective-permute-start | bytes 1966088 | tf_op jit(solution)/shard_map/ppermute | solution.py:32
  130.8 11.5 %collective-permute-start.15 = (bf16[512,640]{1,0:T(8,128)(2,1)S(1)}, bf16[512,640]{1,0:T(8,128)(2,1)S(1)}, u32[]{:S(2)}, u32[]{:S(2)}) collective-permute-start(bf16[512,640]{1,0:T(8,128)(2,1)S(1)} %collective-permute-done.13.a2), channel_id=1, source_target_pairs={{0,1},{1,0},{2,3},{3,2},{4,5},{5,4},{6,7},{7,6},{8,9},{9,8},{10,11... | collective-permute-start | bytes 1966088 | tf_op jit(solution)/shard_map/ppermute | solution.py:32
  (3 other events, 9.8 us)
